TPU v7x, 128 devices: a whole 4x4x4 slice. The times are simulated.
128 devices in a mesh: ctx: 16 (over y, x_hi, core), tp: 8 (over x_lo, z).
Axes of the slice: x: 4 (x_hi: 2, x_lo: 2; x = x_hi * 2 + x_lo), y: 4, z: 4, core: 2. Of those that a mesh axis runs over, the one named last changes fastest.
Arguments:
- query: bfloat16 [16384, 4096], P('ctx', 'tp'), may hold values from -6 to 6
- keys: bfloat16 [16384, 4096], P('ctx', 'tp'), may hold values from -6 to 6
- values: bfloat16 [16384, 4096], P('ctx', 'tp'), may hold values from -6 to 6
- residues: float32 [256, 16], replicated, may hold values from -1.5 to 1.5
- rates: float32 [256, 16], replicated, as said below
- w_out: bfloat16 [4096, 4096], P('tp'), may hold values from -0.125 to 0.125
Outputs:
- mixed: bfloat16 [16384, 4096], P('ctx', 'tp')
Inputs may be any that keep to these rules, and one draw needn't show every extreme that they name: `rates`: each rate lies between 0.25 / 16384 and 1 / 32.
All inputs are finite; a program needn't handle non-finite values.
Results may differ from a plain program's by a relative error of at most 0.015.
Values may be sent and summed in bfloat16 or wider, within the bound.
No kernel may reach another device: no remote copies, remote signals or barrier semaphores. Data moves between devices by JAX's collectives and lax.ppermute only.
A program may use at most 64 MiB of HBM per device.

v0:
```python
import functools
import jax
import jax.numpy as jnp
from jax import lax
from jax.experimental import pallas as pl
from jax.experimental.pallas import tpu as pltpu
from jax.sharding import PartitionSpec as P


SHARE = 16
STATE = 16
CHUNK = 128
PARTS = (128, 256, 128)
SHARED = 64
LIMIT = 12 * 2**20
SPAN = 1024
LANES = 128
PACK = LANES // SHARE


def as_row(spread):
    state = lax.broadcasted_iota(jnp.int32, spread.shape, 0)
    slot = lax.broadcasted_iota(jnp.int32, spread.shape, 1) % STATE
    return jnp.sum(jnp.where(state == slot, spread, 0.0), axis=0, keepdims=True)


def same_group():
    left = lax.broadcasted_iota(jnp.int32, (LANES, LANES), 0) // STATE
    right = lax.broadcasted_iota(jnp.int32, (LANES, LANES), 1) // SHARE
    return left == right


def spread_modes(modes, width):
    groups = modes.shape[1]
    first = lax.axis_index("tp") * (width // SHARE)
    group = lax.broadcasted_iota(jnp.int32, (groups, width), 0) - first
    owner = lax.broadcasted_iota(jnp.int32, (groups, width), 1) // SHARE
    return exact_dot(modes, (group == owner).astype(jnp.float32), 0)


def exact_dot(left, right, side):
    return lax.dot_general(
        left, right, (((1,), (side,)), ((), ())),
        precision=lax.Precision.HIGHEST, preferred_element_type=jnp.float32,
    )


def as_column(modes, width):
    groups = modes.shape[1]
    first = lax.axis_index("tp") * (width // SHARE)
    group = lax.broadcasted_iota(jnp.int32, (width, groups), 1) - first
    owner = lax.broadcasted_iota(jnp.int32, (width, groups), 0) // STATE
    wide = exact_dot((group == owner).astype(jnp.float32), modes, 1)
    slot = lax.broadcasted_iota(jnp.int32, wide.shape, 0) % STATE
    state = lax.broadcasted_iota(jnp.int32, wide.shape, 1)
    return jnp.sum(jnp.where(state == slot, wide, 0.0), axis=1, keepdims=True)


def state_kernel(
    modes_ref, keys_ref, values_ref,
    states_ref, last_ref, spread_ref, leaving_ref, taps_ref, product_ref,
):
    length, width = keys_ref.shape
    chunks = length // CHUNK
    rates = modes_ref[:STATE]
    spread = spread_modes(rates, width)
    spread_ref[...] = spread
    column = as_column(rates, width)
    step = jnp.exp(-float(CHUNK) * spread)
    ahead = (CHUNK - 1 - lax.broadcasted_iota(jnp.int32, (LANES, CHUNK), 1)).astype(jnp.float32)
    keep = same_group()
    gains = modes_ref[STATE:] * jnp.sqrt(2.0 * rates)
    rate_row = as_row(spread)
    gain_row = as_row(spread_modes(gains, width))
    after = (1 + lax.broadcasted_iota(jnp.int32, (CHUNK, width), 0)).astype(jnp.float32)
    leaving_ref[...] = (gain_row * jnp.exp(-rate_row * after)).astype(jnp.bfloat16)
    fadings = []
    for block in range(width // LANES):
        cut = slice(block * LANES, (block + 1) * LANES)
        fading = jnp.exp(-column[cut] * ahead)
        fadings.append(fading)
        fading = fading.astype(jnp.bfloat16)
        decay = step[:, cut]
        carried = jnp.zeros((STATE, LANES), jnp.float32)
        for chunk in range(chunks):
            rows = slice(chunk * CHUNK, (chunk + 1) * CHUNK)
            product = (
                keys_ref[rows, cut].astype(jnp.float32) * values_ref[rows, cut].astype(jnp.float32)
            ).astype(jnp.bfloat16)
            product_ref[rows, cut] = product
            full = jnp.dot(fading, product, preferred_element_type=jnp.float32)
            state = jnp.sum(jnp.where(keep, full, 0.0).reshape(PACK, STATE, LANES), axis=0)
            states_ref[chunk * STATE : (chunk + 1) * STATE, cut] = state
            carried = carried * decay + state
        last_ref[:, cut] = carried
    causal = lax.broadcasted_iota(jnp.int32, (CHUNK, CHUNK), 0) >= lax.broadcasted_iota(
        jnp.int32, (CHUNK, CHUNK), 1
    )
    for block in range(width // LANES):
        cut = slice(block * LANES, (block + 1) * LANES)
        entering = (fadings[block] * jnp.exp(column[cut] * float(CHUNK))).astype(jnp.bfloat16)
        leaving = leaving_ref[:, cut]
        for group in range(PACK):
            at = group * SHARE
            rows = [entering[at : at + SHARE]]
            if group:
                rows.insert(0, jnp.zeros((at, CHUNK), jnp.bfloat16))
            if group < PACK - 1:
                rows.append(jnp.zeros((LANES - at - SHARE, CHUNK), jnp.bfloat16))
            taps = jnp.dot(
                leaving, jnp.concatenate(rows, axis=0), preferred_element_type=jnp.float32
            )
            index = block * PACK + group
            taps_ref[index * CHUNK : (index + 1) * CHUNK, :] = jnp.where(causal, taps, 0.0).astype(
                jnp.bfloat16
            )


def join_kernel(spread_ref, last_ref, one_ref, two_ref, three_ref, total_ref, before_ref, again_ref):
    span = float(SPAN)
    spread = spread_ref[...]
    again_ref[...] = spread
    mine = lax.axis_index("ctx") % 4
    total = last_ref[...] * jnp.exp(-span * (3 - mine).astype(jnp.float32) * spread)
    before = jnp.zeros_like(total)
    for k, ref in ((1, one_ref), (2, two_ref), (3, three_ref)):
        near = ref[...]
        source = mine ^ k
        total = total + near * jnp.exp(-span * (3 - source).astype(jnp.float32) * spread)
        gap = jnp.maximum(mine - source - 1, 0).astype(jnp.float32)
        before = before + jnp.where(mine > source, near * jnp.exp(-span * gap * spread), 0.0)
    total_ref[...] = total
    before_ref[...] = before


def convolve_half(start, taps_ref, product_ref, turned_ref, put):
    rows = product_ref.shape[0] // 2
    chunks = rows // CHUNK
    for block in range(product_ref.shape[1] // LANES):
        cut = slice(block * LANES, (block + 1) * LANES)
        turned = product_ref[pl.ds(start, rows), cut].T
        for group in range(PACK):
            at = group * SHARE
            index = block * PACK + group
            stacked = jnp.concatenate(
                [turned[at : at + SHARE, c * CHUNK : (c + 1) * CHUNK] for c in range(chunks)], axis=0
            )
            folded = lax.dot_general(
                stacked,
                taps_ref[index * CHUNK : (index + 1) * CHUNK, :],
                (((1,), (1,)), ((), ())),
                preferred_element_type=jnp.float32,
            ).astype(jnp.bfloat16)
            for c in range(chunks):
                turned_ref[block, at : at + SHARE, c * CHUNK : (c + 1) * CHUNK] = (
                    folded[c * SHARE : (c + 1) * SHARE]
                )
        put(cut, turned_ref[block].T)


def gate_half(
    half, spread_ref, leaving_ref, query_ref, states_ref, before_ref, above_refs, local, put
):
    length, width = query_ref.shape
    chunks = length // CHUNK // 2
    span = float(SPAN)
    mine = lax.axis_index("ctx") % 4
    spread = spread_ref[...]
    step = jnp.exp(-float(CHUNK) * spread)
    group_step = jnp.exp(-4.0 * span * spread)
    one, two, three = [ref[...] for ref in above_refs]
    above = one + group_step * (two + group_step * three)
    entry = before_ref[...] + above * jnp.exp(-span * mine.astype(jnp.float32) * spread)
    keep = same_group()
    moved = entry
    for chunk in range(chunks):
        moved = moved * step + states_ref[chunk * STATE : (chunk + 1) * STATE, :]
    entry = jnp.where(half == 1, moved, entry)
    start = pl.multiple_of(half * (length // 2), length // 2)
    states = states_ref[pl.ds(pl.multiple_of(half * chunks * STATE, chunks * STATE), chunks * STATE), :]
    for block in range(width // LANES):
        cut = slice(block * LANES, (block + 1) * LANES)
        leaving = leaving_ref[:, cut]
        carried = entry[:, cut]
        near = local(cut)
        query = query_ref[pl.ds(start, length // 2), cut]
        for chunk in range(chunks):
            rows = slice(chunk * CHUNK, (chunk + 1) * CHUNK)
            tall = jnp.concatenate([carried] * PACK, axis=0)
            tall = jnp.where(keep, tall, 0.0).astype(jnp.bfloat16)
            earlier = jnp.dot(leaving, tall, preferred_element_type=jnp.float32)
            convolved = (near[rows].astype(jnp.float32) + earlier).astype(jnp.bfloat16)
            gated = query[rows].astype(jnp.float32) * convolved.astype(jnp.float32)
            put(chunk, cut, gated.astype(jnp.bfloat16))
            carried = carried * step[:, cut] + states[chunk * STATE : (chunk + 1) * STATE, cut]


def other_half():
    return 1 - lax.axis_index("tp") // 4


def near_kernel(taps_ref, product_ref, out_ref, turned_ref):
    rows = out_ref.shape[0]
    start = pl.multiple_of(other_half() * rows, rows)

    def put(cut, value):
        out_ref[:, cut] = value

    convolve_half(start, taps_ref, product_ref, turned_ref, put)


def send_kernel(
    spread_ref, leaving_ref, query_ref, near_ref, states_ref, before_ref,
    one_ref, two_ref, three_ref, *out_refs,
):
    homes = [(ref, row) for ref in out_refs for row in range(0, ref.shape[0], CHUNK)]

    def put(chunk, cut, value):
        ref, row = homes[chunk]
        ref[row : row + CHUNK, cut] = value

    gate_half(
        other_half(), spread_ref, leaving_ref, query_ref, states_ref, before_ref,
        (one_ref, two_ref, three_ref), lambda cut: near_ref[:, cut], put,
    )


def keep_kernel(
    spread_ref, leaving_ref, query_ref, taps_ref, product_ref, states_ref, before_ref,
    one_ref, two_ref, three_ref, out_ref, turned_ref, near_ref,
):
    half = 1 - other_half()
    rows = near_ref.shape[0]

    def put_near(cut, value):
        near_ref[:, cut] = value

    def put(chunk, cut, value):
        out_ref[chunk * CHUNK : (chunk + 1) * CHUNK, cut] = value

    convolve_half(
        pl.multiple_of(half * rows, rows), taps_ref, product_ref, turned_ref, put_near
    )
    gate_half(
        half, spread_ref, leaving_ref, query_ref, states_ref, before_ref,
        (one_ref, two_ref, three_ref), lambda cut: near_ref[:, cut], put,
    )


def vmem():
    return pl.BlockSpec(memory_space=pltpu.VMEM)


def anywhere():
    return pl.BlockSpec(memory_space=pl.ANY)


def cost(us):
    return pl.CostEstimate(flops=0, transcendentals=0, bytes_accessed=int(us * 3.0e6))


def call(kernel, us, out_shape, *args, scratch=()):
    return pl.pallas_call(
        kernel,
        out_shape=out_shape,
        in_specs=[vmem()] * len(args),
        out_specs=jax.tree.map(lambda _: vmem(), out_shape),
        scratch_shapes=list(scratch),
        cost_estimate=cost(us),
        compiler_params=pltpu.CompilerParams(vmem_limit_bytes=LIMIT),
    )(*args)


def route(change):
    pairs = []
    for index in range(128):
        ctx, tp = divmod(index, 8)
        spot = {"y": ctx // 4, "far": ctx // 2 % 2, "core": ctx % 2, "near": tp // 4, "z": tp % 4}
        spot.update(change(spot))
        there = spot["y"] * 4 + spot["far"] * 2 + spot["core"]
        pairs.append((index, there * 8 + spot["near"] * 4 + spot["z"]))
    return pairs


def move(array, change):
    return lax.ppermute(array, ("ctx", "tp"), route(change))


def along(axis, size, by):
    return lambda spot: {axis: (spot[axis] + by) % size}


def either_side(spot):
    x = spot["far"] * 2 + spot["near"]
    step = 1 if x % 2 == spot["core"] else -1
    x = (x + step) % 4
    return {"far": x // 2, "near": x % 2}


def column_blocks(steps):
    tp = lax.axis_index("tp")
    near, z = tp // 4, tp % 4
    return [((1 - near) * 4 if other else near * 4) + ((z + step) & 3) for step, other in steps]


def slab_kernel(w_ref, shared_ref, common_ref, sems):
    ctx = lax.axis_index("ctx")
    row = pl.multiple_of(ctx % 2 * 256, 256)
    odd = pl.multiple_of(row + ctx // 4 % 2 * SHARED, SHARED)
    common = common_ref.shape[0]
    copies = [
        pltpu.make_async_copy(w_ref.at[pl.ds(odd, SHARED)], shared_ref, sems.at[0]),
        pltpu.make_async_copy(w_ref.at[pl.ds(row + 2 * SHARED, common)], common_ref, sems.at[1]),
    ]
    for copy in copies:
        copy.start()
    for copy in copies:
        copy.wait()


def cut_slabs(w_out):
    return pl.pallas_call(
        slab_kernel,
        out_shape=[
            jax.ShapeDtypeStruct((rows, w_out.shape[1]), w_out.dtype)
            for rows in (SHARED, 256 - 2 * SHARED)
        ],
        in_specs=[anywhere()],
        out_specs=[vmem()] * 2,
        scratch_shapes=[pltpu.SemaphoreType.DMA((2,))],
        cost_estimate=cost(1),
        compiler_params=pltpu.CompilerParams(vmem_limit_bytes=60 * 2**20),
    )(w_out)


def gather_kernel(*refs):
    piece_refs, out_ref, sems = refs[:-2], refs[-2], refs[-1]
    ctx = lax.axis_index("ctx")
    core, odd = ctx % 2, ctx // 4 % 2
    offsets = (odd * SHARED, (1 - odd) * SHARED, (1 - odd) * SHARED + SHARED // 2, 2 * SHARED)
    copies = []
    for index, piece in enumerate(piece_refs):
        half = core if index < 4 else 1 - core
        row = pl.multiple_of(half * 256 + offsets[index % 4], SHARED // 2)
        copies.append(
            pltpu.make_async_copy(piece, out_ref.at[pl.ds(row, piece.shape[0])], sems.at[index])
        )
        copies[-1].start()
    for copy in copies:
        copy.wait()


def gather(pieces):
    return pl.pallas_call(
        gather_kernel,
        out_shape=jax.ShapeDtypeStruct((512, pieces[0].shape[1]), jnp.bfloat16),
        in_specs=[anywhere()] * len(pieces),
        out_specs=vmem(),
        scratch_shapes=[pltpu.SemaphoreType.DMA((len(pieces),))],
        cost_estimate=cost(2),
        compiler_params=pltpu.CompilerParams(vmem_limit_bytes=LIMIT),
    )(*pieces)


def project_kernel(steps, start, *refs):
    mine_ref, theirs_ref, own_ref, got_ref = refs[:4]
    out_refs = refs[4:]
    rows = theirs_ref.shape[0]
    mine = mine_ref[start : start + rows]
    theirs = theirs_ref[...]
    for out_ref, block in zip(out_refs, column_blocks(steps)):
        columns = pl.ds(pl.multiple_of(block * 512, 512), 512)
        total = jnp.dot(mine, own_ref[:, columns], preferred_element_type=jnp.float32)
        total += jnp.dot(theirs, got_ref[:, columns], preferred_element_type=jnp.float32)
        out_ref[...] = total.astype(jnp.bfloat16)


def project(steps, start, mine, theirs, own, got):
    count = len(steps)
    out = jax.ShapeDtypeStruct(theirs.shape, jnp.bfloat16)
    return call(
        functools.partial(project_kernel, steps, start), count, [out] * count, mine, theirs, own, got
    )


def finish_kernel(*refs):
    out_ref = refs[-1]
    near = lax.axis_index("tp") // 4
    start = 0
    for part, rows in enumerate(PARTS):
        own = refs[part]
        right, left, swapped = refs[len(PARTS) + part * 3 : len(PARTS) + part * 3 + 3]
        total = own[...].astype(jnp.float32) + right[...].astype(jnp.float32)
        total = (total + left[...].astype(jnp.float32)).astype(jnp.bfloat16)
        here = pl.multiple_of(near * sum(PARTS) + start, CHUNK)
        there = pl.multiple_of((1 - near) * sum(PARTS) + start, CHUNK)
        out_ref[pl.ds(here, rows), :] = total
        out_ref[pl.ds(there, rows), :] = swapped[...]
        start += rows


def plus(*arrays):
    total = arrays[0].astype(jnp.float32)
    for array in arrays[1:]:
        total = total + array.astype(jnp.float32)
    return total.astype(jnp.bfloat16)


def layer(query, keys, values, residues, rates, w_out):
    length, width = keys.shape
    shape = jax.ShapeDtypeStruct

    modes = jnp.concatenate([rates.T, residues.T])
    shared, common = cut_slabs(w_out)
    shared = move(shared, either_side)
    common = move(common, either_side)
    fetched = [
        shared,
        move(shared[: SHARED // 2], along("y", 4, 1)),
        move(shared[SHARED // 2 :], along("y", 4, -1)),
        common,
    ]

    small = shape((STATE, width), jnp.float32)
    states, last, spread, leaving, taps, product = call(
        state_kernel,
        3,
        (
            shape((length // CHUNK * STATE, width), jnp.float32),
            small,
            small,
            shape((CHUNK, width), jnp.bfloat16),
            shape((width // SHARE * CHUNK, CHUNK), jnp.bfloat16),
            shape(keys.shape, jnp.bfloat16),
        ),
        modes, keys, values,
    )
    near = []
    for k in range(1, 4):
        pairs = [(c, c ^ k) for c in range(16)]
        near.append(lax.ppermute(last, "ctx", pairs))
    total, before, spread = call(join_kernel, 1, (small, small, small), spread, last, *near)
    above = [
        lax.ppermute(total, "ctx", [(c, c + 4 * k) for c in range(16 - 4 * k)])
        for k in range(1, 4)
    ]
    tall = shape((length // 2, width), jnp.bfloat16)
    turned = pltpu.VMEM((width // LANES, LANES, length // 2), jnp.bfloat16)
    local = call(near_kernel, 3, tall, taps, product, scratch=[turned])
    above, local = lax.optimization_barrier((above, local))
    others = call(
        send_kernel, 2, [shape((rows, width), jnp.bfloat16) for rows in PARTS],
        spread, leaving, query, local, states, before, *above,
    )
    theirs = [move(other, along("near", 2, 1)) for other in others]
    mine = call(
        keep_kernel, 4, tall,
        spread, leaving, query, taps, product, states, before, *above,
        scratch=[turned, pltpu.VMEM((length // 2, width), jnp.bfloat16)],
    )
    common, others = lax.optimization_barrier((common, others))
    fetched[3] = common
    swapped = [move(piece, along("core", 2, 1)) for piece in fetched]
    pieces = fetched + swapped
    got = gather(pieces)

    finals, rest = [], []
    for part in range(len(PARTS)):
        start = sum(PARTS[:part])
        if part:
            theirs[part], free = lax.optimization_barrier((theirs[part], free))
        args = (start, mine, theirs[part], w_out, got)
        far = ((2, True), (2, False))
        near_free = ((1, False), (-1, True))
        rest_steps = ((1, True), (-1, False), (0, True), (0, False))
        first = far if part else far + near_free
        last_ones = near_free + rest_steps if part else rest_steps
        blocks = project(first, *args)
        blocks += project(last_ones, *args)
        far_p, far_o, right_o, left_p, right_p, left_o, own_p, own_o = blocks
        finals.append(own_o)
        free = right_o
        far_p = move(far_p, along("z", 4, 1))
        far_o = move(far_o, along("z", 4, -1))
        right_o = move(right_o, along("z", 4, 1))
        left_p = move(left_p, along("z", 4, -1))
        right_p = move(plus(right_p, far_p), along("z", 4, 1))
        left_o = move(plus(left_o, far_o), along("z", 4, -1))
        swapped = move(plus(own_p, right_p, left_p), along("near", 2, 1))
        rest += [right_o, left_o, swapped]
    return call(finish_kernel, 1, shape((length, 512), jnp.bfloat16), *finals, *rest)


def solution(mesh):
    in_specs = (P("ctx", "tp"), P("ctx", "tp"), P("ctx", "tp"), P(), P(), P("tp", None))
    return jax.shard_map(
        layer, mesh=mesh, in_specs=in_specs, out_specs=P("ctx", "tp"), check_vma=False
    )
```

profile of v0, /device:TPU:0, one launch (start us, length us, event | category | flops | bytes accessed | tf_op | source)
XLA Modules:
  0.0 123.0 jit_solution(6383956969140672582)
XLA Ops:
  0.0 2.7 %shard_map.69 = (bf16[64,4096]{1,0:T(8,128)(2,1)}, bf16[128,4096]{1,0:T(8,128)(2,1)}) custom-call(bf16[512,4096]{1,0:T(8,128)(2,1)} %refs_2_.11), custom_call_target="tpu_custom_call" | custom-call | bytes 3000000 | tf_op jit(solution)/shard_map/pallas_call | solution.py:322
  2.7 1.7 %collective-permute-start.10 = (bf16[128,4096]{1,0:T(8,128)(2,1)}, bf16[128,4096]{1,0:T(8,128)(2,1)S(1)}, u32[]{:S(2)}, u32[]{:S(2)}) collective-permute-start(bf16[128,4096]{1,0:T(8,128)(2,1)} %get-tuple-element.65), channel_id=1, source_target_pairs={{0,4},{1,5},{2,6},{3,7},{4,0},{5,1},{6,2},{7,3},{8,28},{9,29},{10,... | collective-permute-start | bytes 3145736 | tf_op jit(solution)/shard_map/ppermute | solution.py:286
  4.9 2.1 %shard_map.64 = (f32[128,512]{1,0:T(8,128)S(1)}, f32[16,512]{1,0:T(8,128)S(1)}, f32[16,512]{1,0:T(8,128)S(1)}, bf16[128,512]{1,0:T(8,128)(2,1)S(1)}, bf16[4096,1...) custom-call(f32[32,256]{1,0:T(8,128)S(1)} %pad_maximum_fusion.modes_ref, bf16[1024,512]{1,0:T(8,128)(2,1)S(1)} %copy-done.2, ...), custom_call_target="tpu_custom_call" | custom-call | bytes 9000000 | tf_op jit(solution)/shard_map/pallas_call | solution.py:263
  7.0 2.1 %collective-permute-start.2 = (f32[16,512]{1,0:T(8,128)S(1)}, f32[16,512]{1,0:T(8,128)S(1)}, u32[]{:S(2)}, u32[]{:S(2)}) collective-permute-start(f32[16,512]{1,0:T(8,128)S(1)} %get-tuple-element.51.last_ref), channel_id=1, source_target_pairs={{0,24},{8,16},{16,8},{24,0},{32,56},{40,48},{48,40},{56,32},{64,88... | collective-permute-start | bytes 98312 | tf_op jit(solution)/shard_map/ppermute | solution.py:441
  9.1 1.6 %collective-permute-start.1 = (f32[16,512]{1,0:T(8,128)S(1)}, f32[16,512]{1,0:T(8,128)S(1)}, u32[]{:S(2)}, u32[]{:S(2)}) collective-permute-start(f32[16,512]{1,0:T(8,128)S(1)} %get-tuple-element.51.last_ref), channel_id=1, source_target_pairs={{0,16},{8,24},{16,0},{24,8},{32,48},{40,56},{48,32},{56,40},{64,80... | collective-permute-start | bytes 98312 | tf_op jit(solution)/shard_map/ppermute | solution.py:441
  10.7 12.9 %collective-permute-done.2.three_ref = f32[16,512]{1,0:T(8,128)S(1)} collective-permute-done((f32[16,512]{1,0:T(8,128)S(1)}, f32[16,512]{1,0:T(8,128)S(1)}, u32[]{:S(2)}, u32[]{:S(2)}) %collective-permute-start.2) | collective-permute-done | bytes 32800 | tf_op jit(solution)/shard_map/ppermute | solution.py:441
  23.6 3.5 %collective-permute-done.1.two_ref = f32[16,512]{1,0:T(8,128)S(1)} collective-permute-done((f32[16,512]{1,0:T(8,128)S(1)}, f32[16,512]{1,0:T(8,128)S(1)}, u32[]{:S(2)}, u32[]{:S(2)}) %collective-permute-start.1) | collective-permute-done | bytes 32800 | tf_op jit(solution)/shard_map/ppermute | solution.py:441
  27.2 4.9 %collective-permute-start.5 = (f32[16,512]{1,0:T(8,128)S(1)}, f32[16,512]{1,0:T(8,128)S(1)}, u32[]{:S(2)}, u32[]{:S(2)}) collective-permute-start(f32[16,512]{1,0:T(8,128)S(1)} %get-tuple-element.58), channel_id=1, source_target_pairs={{0,96},{8,104},{16,112},{24,120},{1,97},{9,105},{17,113},{25,121},... | collective-permute-start | bytes 98312 | tf_op jit(solution)/shard_map/ppermute | solution.py:444
  32.2 1.3 %collective-permute-start.4 = (f32[16,512]{1,0:T(8,128)S(1)}, f32[16,512]{1,0:T(8,128)S(1)}, u32[]{:S(2)}, u32[]{:S(2)}) collective-permute-start(f32[16,512]{1,0:T(8,128)S(1)} %get-tuple-element.58), channel_id=1, source_target_pairs={{0,64},{8,72},{16,80},{24,88},{32,96},{40,104},{48,112},{56,120},{... | collective-permute-start | bytes 98312 | tf_op jit(solution)/shard_map/ppermute | solution.py:444
  33.5 2.8 %collective-permute-start.3 = (f32[16,512]{1,0:T(8,128)S(1)}, f32[16,512]{1,0:T(8,128)S(1)}, u32[]{:S(2)}, u32[]{:S(2)}) collective-permute-start(f32[16,512]{1,0:T(8,128)S(1)} %get-tuple-element.58), channel_id=1, source_target_pairs={{0,32},{8,40},{16,48},{24,56},{32,64},{40,72},{48,80},{56,88},{64,... | collective-permute-start | bytes 98312 | tf_op jit(solution)/shard_map/ppermute | solution.py:444
  36.2 0.9 shard_map.66.near_ref
  37.1 0.7 collective-permute-done.3.one_ref
  38.4 1.1 collective-permute-start.9
  39.5 1.3 %collective-permute-start.8 = (bf16[32,4096]{1,0:T(8,128)(2,1)S(1)}, bf16[32,4096]{1,0:T(8,128)(2,1)S(1)}, u32[]{:S(2)}, u32[]{:S(2)}) collective-permute-start(bf16[32,4096]{1,0:T(8,128)(2,1)S(1)} %get-tuple-element.96), channel_id=1, source_target_pairs={{0,32},{1,33},{2,34},{3,35},{4,36},{5,37},{6,38},{7,39},{8,40},{9,... | collective-permute-start | bytes 786440 | tf_op jit(solution)/shard_map/ppermute | solution.py:286
  41.1 6.7 %collective-permute-done.9.refs_2_ = bf16[32,4096]{1,0:T(8,128)(2,1)S(1)} collective-permute-done((bf16[32,4096]{1,0:T(8,128)(2,1)S(1)}, bf16[32,4096]{1,0:T(8,128)(2,1)S(1)}, u32[]{:S(2)}, u32[]{:S(2)}) %collective-permute-start.9) | collective-permute-done | bytes 262176 | tf_op jit(solution)/shard_map/ppermute | solution.py:286
  47.7 1.4 %collective-permute-done.8.refs_1_ = bf16[32,4096]{1,0:T(8,128)(2,1)S(1)} collective-permute-done((bf16[32,4096]{1,0:T(8,128)(2,1)S(1)}, bf16[32,4096]{1,0:T(8,128)(2,1)S(1)}, u32[]{:S(2)}, u32[]{:S(2)}) %collective-permute-start.8) | collective-permute-done | bytes 262176 | tf_op jit(solution)/shard_map/ppermute | solution.py:286
  49.4 1.8 %collective-permute-start.6 = (bf16[128,512]{1,0:T(8,128)(2,1)S(1)}, bf16[128,512]{1,0:T(8,128)(2,1)S(1)}, u32[]{:S(2)}, u32[]{:S(2)}) collective-permute-start(bf16[128,512]{1,0:T(8,128)(2,1)S(1)} %get-tuple-element.63), channel_id=1, source_target_pairs={{0,4},{1,5},{2,6},{3,7},{4,0},{5,1},{6,2},{7,3},{8,12},{9,13},{10,... | collective-permute-start | bytes 393224 | tf_op jit(solution)/shard_map/ppermute | solution.py:286
  51.4 1.1 shard_map.67.refs_0_
  53.0 8.1 %collective-permute-done.6.refs_1_ = bf16[128,512]{1,0:T(8,128)(2,1)S(1)} collective-permute-done((bf16[128,512]{1,0:T(8,128)(2,1)S(1)}, bf16[128,512]{1,0:T(8,128)(2,1)S(1)}, u32[]{:S(2)}, u32[]{:S(2)}) %collective-permute-start.6) | collective-permute-done | bytes 131104 | tf_op jit(solution)/shard_map/ppermute | solution.py:286
  61.1 0.7 shard_map.72
  61.9 2.0 %collective-permute-start.20 = (bf16[128,512]{1,0:T(8,128)(2,1)S(1)}, bf16[128,512]{1,0:T(8,128)(2,1)S(1)}, u32[]{:S(2)}, u32[]{:S(2)}) collective-permute-start(bf16[128,512]{1,0:T(8,128)(2,1)S(1)} %get-tuple-element.80), channel_id=1, source_target_pairs={{0,1},{1,2},{2,3},{3,0},{4,5},{5,6},{6,7},{7,4},{8,9},{9,10},{10,1... | collective-permute-start | bytes 393224 | tf_op jit(solution)/shard_map/ppermute | solution.py:286
  63.9 1.9 %collective-permute-start.17 = (bf16[128,512]{1,0:T(8,128)(2,1)S(1)}, bf16[128,512]{1,0:T(8,128)(2,1)S(1)}, u32[]{:S(2)}, u32[]{:S(2)}) collective-permute-start(bf16[128,512]{1,0:T(8,128)(2,1)S(1)} %get-tuple-element.70), channel_id=1, source_target_pairs={{0,1},{1,2},{2,3},{3,0},{4,5},{5,6},{6,7},{7,4},{8,9},{9,10},{10,1... | collective-permute-start | bytes 393224 | tf_op jit(solution)/shard_map/ppermute | solution.py:286
  65.8 0.7 shard_map.75
  66.5 1.8 %shard_map.73 = (bf16[256,512]{1,0:T(8,128)(2,1)S(1)}, bf16[256,512]{1,0:T(8,128)(2,1)S(1)}, bf16[256,512]{1,0:T(8,128)(2,1)S(1)}, bf16[256,512]{1,0:T(8,128)(2,...) custom-call(bf16[512,512]{1,0:T(8,128)(2,1)S(1)} %shard_map.67.refs_0_, ...), custom_call_target="tpu_custom_call" | custom-call | bytes 18000000 | tf_op jit(solution)/shard_map/pallas_call | solution.py:263
  68.8 1.0 shard_map.74
  69.8 1.4 %collective-permute-start.18 = (bf16[128,512]{1,0:T(8,128)(2,1)S(1)}, bf16[128,512]{1,0:T(8,128)(2,1)S(1)}, u32[]{:S(2)}, u32[]{:S(2)}) collective-permute-start(bf16[128,512]{1,0:T(8,128)(2,1)S(1)} %get-tuple-element.77), channel_id=1, source_target_pairs={{0,3},{1,0},{2,1},{3,2},{4,7},{5,4},{6,5},{7,6},{8,11},{9,8},{10,9... | collective-permute-start | bytes 393224 | tf_op jit(solution)/shard_map/ppermute | solution.py:286
  71.2 1.2 collective-permute-start.22
  72.4 1.8 %collective-permute-start.25 = (bf16[256,512]{1,0:T(8,128)(2,1)S(1)}, bf16[256,512]{1,0:T(8,128)(2,1)S(1)}, u32[]{:S(2)}, u32[]{:S(2)}) collective-permute-start(bf16[256,512]{1,0:T(8,128)(2,1)S(1)} %get-tuple-element.83), channel_id=1, source_target_pairs={{0,3},{1,0},{2,1},{3,2},{4,7},{5,4},{6,5},{7,6},{8,11},{9,8},{10,9... | collective-permute-start | bytes 786440 | tf_op jit(solution)/shard_map/ppermute | solution.py:286
  74.1 0.7 shard_map.71
  75.3 1.0 collective-permute-done.18
  76.3 2.5 %collective-permute-start.32 = (bf16[128,512]{1,0:T(8,128)(2,1)S(1)}, bf16[128,512]{1,0:T(8,128)(2,1)S(1)}, u32[]{:S(2)}, u32[]{:S(2)}) collective-permute-start(bf16[128,512]{1,0:T(8,128)(2,1)S(1)} %get-tuple-element.90), channel_id=1, source_target_pairs={{0,3},{1,0},{2,1},{3,2},{4,7},{5,4},{6,5},{7,6},{8,11},{9,8},{10,9... | collective-permute-start | bytes 393224 | tf_op jit(solution)/shard_map/ppermute | solution.py:286
  78.8 6.3 %collective-permute-done.32 = bf16[128,512]{1,0:T(8,128)(2,1)S(1)} collective-permute-done((bf16[128,512]{1,0:T(8,128)(2,1)S(1)}, bf16[128,512]{1,0:T(8,128)(2,1)S(1)}, u32[]{:S(2)}, u32[]{:S(2)}) %collective-permute-start.32) | collective-permute-done | bytes 131104 | tf_op jit(solution)/shard_map/ppermute | solution.py:286
  85.2 1.6 %collective-permute-start.34 = (bf16[128,512]{1,0:T(8,128)(2,1)S(1)}, bf16[128,512]{1,0:T(8,128)(2,1)S(1)}, u32[]{:S(2)}, u32[]{:S(2)}) collective-permute-start(bf16[128,512]{1,0:T(8,128)(2,1)S(1)} %get-tuple-element.93), channel_id=1, source_target_pairs={{0,1},{1,2},{2,3},{3,0},{4,5},{5,6},{6,7},{7,4},{8,9},{9,10},{10,1... | collective-permute-start | bytes 393224 | tf_op jit(solution)/shard_map/ppermute | solution.py:286
  86.8 4.5 %collective-permute-done.34 = bf16[128,512]{1,0:T(8,128)(2,1)S(1)} collective-permute-done((bf16[128,512]{1,0:T(8,128)(2,1)S(1)}, bf16[128,512]{1,0:T(8,128)(2,1)S(1)}, u32[]{:S(2)}, u32[]{:S(2)}) %collective-permute-start.34) | collective-permute-done | bytes 131104 | tf_op jit(solution)/shard_map/ppermute | solution.py:286
  91.3 1.8 %collective-permute-start.29 = (bf16[256,512]{1,0:T(8,128)(2,1)S(1)}, bf16[256,512]{1,0:T(8,128)(2,1)S(1)}, u32[]{:S(2)}, u32[]{:S(2)}) collective-permute-start(bf16[256,512]{1,0:T(8,128)(2,1)S(1)} %get-tuple-element.87), channel_id=1, source_target_pairs={{0,3},{1,0},{2,1},{3,2},{4,7},{5,4},{6,5},{7,6},{8,11},{9,8},{10,9... | collective-permute-start | bytes 786440 | tf_op jit(solution)/shard_map/ppermute | solution.py:286
  94.1 0.8 collective-permute-start.24
  94.9 5.9 %collective-permute-done.21 = bf16[128,512]{1,0:T(8,128)(2,1)S(1)} collective-permute-done((bf16[128,512]{1,0:T(8,128)(2,1)S(1)}, bf16[128,512]{1,0:T(8,128)(2,1)S(1)}, u32[]{:S(2)}, u32[]{:S(2)}) %collective-permute-start.21) | collective-permute-done | bytes 131104 | tf_op jit(solution)/shard_map/ppermute | solution.py:286
  100.9 3.3 %collective-permute-start.36 = (bf16[128,512]{1,0:T(8,128)(2,1)S(1)}, bf16[128,512]{1,0:T(8,128)(2,1)S(1)}, u32[]{:S(2)}, u32[]{:S(2)}) collective-permute-start(bf16[128,512]{1,0:T(8,128)(2,1)S(1)} %get-tuple-element.94), channel_id=1, source_target_pairs={{0,3},{1,0},{2,1},{3,2},{4,7},{5,4},{6,5},{7,6},{8,11},{9,8},{10,9... | collective-permute-start | bytes 393224 | tf_op jit(solution)/shard_map/ppermute | solution.py:286
  104.2 2.2 %collective-permute-done.28 = bf16[256,512]{1,0:T(8,128)(2,1)S(1)} collective-permute-done((bf16[256,512]{1,0:T(8,128)(2,1)S(1)}, bf16[256,512]{1,0:T(8,128)(2,1)S(1)}, u32[]{:S(2)}, u32[]{:S(2)}) %collective-permute-start.28) | collective-permute-done | bytes 262176 | tf_op jit(solution)/shard_map/ppermute | solution.py:286
  106.5 3.3 %collective-permute-start.19 = (bf16[128,512]{1,0:T(8,128)(2,1)S(1)}, bf16[128,512]{1,0:T(8,128)(2,1)S(1)}, u32[]{:S(2)}, u32[]{:S(2)}) collective-permute-start(bf16[128,512]{1,0:T(8,128)(2,1)S(1)} %add_convert_fusion.8), channel_id=1, source_target_pairs={{0,3},{1,0},{2,1},{3,2},{4,7},{5,4},{6,5},{7,6},{8,11},{9,8},{10,9... | collective-permute-start | bytes 393224 | tf_op jit(solution)/shard_map/ppermute | solution.py:286
  109.8 0.5 collective-permute-start.26
  110.3 2.2 %collective-permute-done.35 = bf16[128,512]{1,0:T(8,128)(2,1)S(1)} collective-permute-done((bf16[128,512]{1,0:T(8,128)(2,1)S(1)}, bf16[128,512]{1,0:T(8,128)(2,1)S(1)}, u32[]{:S(2)}, u32[]{:S(2)}) %collective-permute-start.35) | collective-permute-done | bytes 131104 | tf_op jit(solution)/shard_map/ppermute | solution.py:286
  113.1 0.6 collective-permute-start.33
  113.7 1.6 %collective-permute-start.23 = (bf16[128,512]{1,0:T(8,128)(2,1)S(1)}, bf16[128,512]{1,0:T(8,128)(2,1)S(1)}, u32[]{:S(2)}, u32[]{:S(2)}) collective-permute-start(bf16[128,512]{1,0:T(8,128)(2,1)S(1)} %add_convert_fusion.6), channel_id=1, source_target_pairs={{0,4},{1,5},{2,6},{3,7},{4,0},{5,1},{6,2},{7,3},{8,12},{9,13},{10,... | collective-permute-start | bytes 393224 | tf_op jit(solution)/shard_map/ppermute | solution.py:286
  115.7 2.4 %collective-permute-done.33.refs_10_ = bf16[128,512]{1,0:T(8,128)(2,1)S(1)} collective-permute-done((bf16[128,512]{1,0:T(8,128)(2,1)S(1)}, bf16[128,512]{1,0:T(8,128)(2,1)S(1)}, u32[]{:S(2)}, u32[]{:S(2)}) %collective-permute-start.33) | collective-permute-done | bytes 131104 | tf_op jit(solution)/shard_map/ppermute | solution.py:286
  118.2 2.2 %collective-permute-done.23.refs_5_ = bf16[128,512]{1,0:T(8,128)(2,1)S(1)} collective-permute-done((bf16[128,512]{1,0:T(8,128)(2,1)S(1)}, bf16[128,512]{1,0:T(8,128)(2,1)S(1)}, u32[]{:S(2)}, u32[]{:S(2)}) %collective-permute-start.23) | collective-permute-done | bytes 131104 | tf_op jit(solution)/shard_map/ppermute | solution.py:286
  120.4 1.4 %collective-permute-done.37.refs_11_ = bf16[128,512]{1,0:T(8,128)(2,1)S(1)} collective-permute-done((bf16[128,512]{1,0:T(8,128)(2,1)S(1)}, bf16[128,512]{1,0:T(8,128)(2,1)S(1)}, u32[]{:S(2)}, u32[]{:S(2)}) %collective-permute-start.37) | collective-permute-done | bytes 131104 | tf_op jit(solution)/shard_map/ppermute | solution.py:286
  121.8 1.2 shard_map.77
  (65 shorter events, 5.2 us)
Async XLA Ops:
  0.0 4.8 %copy-start.5 = (f32[256,16]{0,1:T(8,128)S(1)}, f32[256,16]{0,1:T(8,128)}, u32[]{:S(2)}) copy-start(f32[256,16]{0,1:T(8,128)} %param.10) | copy-start | bytes 49156
  0.0 4.8 %copy-start.4 = (f32[256,16]{0,1:T(8,128)S(1)}, f32[256,16]{0,1:T(8,128)}, u32[]{:S(2)}) copy-start(f32[256,16]{0,1:T(8,128)} %param.9) | copy-start | bytes 49156
  0.0 4.9 %copy-start.3 = (bf16[1024,512]{1,0:T(8,128)(2,1)S(1)}, bf16[1024,512]{1,0:T(8,128)(2,1)}, u32[]{:S(2)}) copy-start(bf16[1024,512]{1,0:T(8,128)(2,1)} %values_ref.1) | copy-start | bytes 3145732
  0.0 4.9 %copy-start.2 = (bf16[1024,512]{1,0:T(8,128)(2,1)S(1)}, bf16[1024,512]{1,0:T(8,128)(2,1)}, u32[]{:S(2)}) copy-start(bf16[1024,512]{1,0:T(8,128)(2,1)} %keys_ref.1) | copy-start | bytes 3145732
  0.0 37.8 %copy-start.1 = (bf16[1024,512]{1,0:T(8,128)(2,1)S(1)}, bf16[1024,512]{1,0:T(8,128)(2,1)}, u32[]{:S(2)}) copy-start(bf16[1024,512]{1,0:T(8,128)(2,1)} %query_ref.3) | copy-start | bytes 3145732
  2.7 35.5 %collective-permute-start.10 = (bf16[128,4096]{1,0:T(8,128)(2,1)}, bf16[128,4096]{1,0:T(8,128)(2,1)S(1)}, u32[]{:S(2)}, u32[]{:S(2)}) collective-permute-start(bf16[128,4096]{1,0:T(8,128)(2,1)} %get-tuple-element.65), channel_id=1, source_target_pairs={{0,4},{1,5},{2,6},{3,7},{4,0},{5,1},{6,2},{7,3},{8,28},{9,29},{10,... | collective-permute-start | bytes 3145736 | tf_op jit(solution)/shard_map/ppermute | solution.py:286
  4.4 33.9 %collective-permute-start.7 = (bf16[64,4096]{1,0:T(8,128)(2,1)}, bf16[64,4096]{1,0:T(8,128)(2,1)S(1)}, u32[]{:S(2)}, u32[]{:S(2)}) collective-permute-start(bf16[64,4096]{1,0:T(8,128)(2,1)} %get-tuple-element.64), channel_id=1, source_target_pairs={{0,4},{1,5},{2,6},{3,7},{4,0},{5,1},{6,2},{7,3},{8,28},{9,29},{10,... | collective-permute-start | bytes 1572872 | tf_op jit(solution)/shard_map/ppermute | solution.py:286
  7.0 16.6 %collective-permute-start.2 = (f32[16,512]{1,0:T(8,128)S(1)}, f32[16,512]{1,0:T(8,128)S(1)}, u32[]{:S(2)}, u32[]{:S(2)}) collective-permute-start(f32[16,512]{1,0:T(8,128)S(1)} %get-tuple-element.51.last_ref), channel_id=1, source_target_pairs={{0,24},{8,16},{16,8},{24,0},{32,56},{40,48},{48,40},{56,32},{64,88... | collective-permute-start | bytes 98312 | tf_op jit(solution)/shard_map/ppermute | solution.py:441
  9.1 18.0 %collective-permute-start.1 = (f32[16,512]{1,0:T(8,128)S(1)}, f32[16,512]{1,0:T(8,128)S(1)}, u32[]{:S(2)}, u32[]{:S(2)}) collective-permute-start(f32[16,512]{1,0:T(8,128)S(1)} %get-tuple-element.51.last_ref), channel_id=1, source_target_pairs={{0,16},{8,24},{16,0},{24,8},{32,48},{40,56},{48,32},{56,40},{64,80... | collective-permute-start | bytes 98312 | tf_op jit(solution)/shard_map/ppermute | solution.py:441
  10.7 16.4 %collective-permute-start = (f32[16,512]{1,0:T(8,128)S(1)}, f32[16,512]{1,0:T(8,128)S(1)}, u32[]{:S(2)}, u32[]{:S(2)}) collective-permute-start(f32[16,512]{1,0:T(8,128)S(1)} %get-tuple-element.51.last_ref), channel_id=1, source_target_pairs={{0,8},{8,0},{16,24},{24,16},{32,40},{40,32},{48,56},{56,48},{64,72... | collective-permute-start | bytes 98312 | tf_op jit(solution)/shard_map/ppermute | solution.py:441
  27.2 9.9 %collective-permute-start.5 = (f32[16,512]{1,0:T(8,128)S(1)}, f32[16,512]{1,0:T(8,128)S(1)}, u32[]{:S(2)}, u32[]{:S(2)}) collective-permute-start(f32[16,512]{1,0:T(8,128)S(1)} %get-tuple-element.58), channel_id=1, source_target_pairs={{0,96},{8,104},{16,112},{24,120},{1,97},{9,105},{17,113},{25,121},... | collective-permute-start | bytes 98312 | tf_op jit(solution)/shard_map/ppermute | solution.py:444
  32.2 5.0 %collective-permute-start.4 = (f32[16,512]{1,0:T(8,128)S(1)}, f32[16,512]{1,0:T(8,128)S(1)}, u32[]{:S(2)}, u32[]{:S(2)}) collective-permute-start(f32[16,512]{1,0:T(8,128)S(1)} %get-tuple-element.58), channel_id=1, source_target_pairs={{0,64},{8,72},{16,80},{24,88},{32,96},{40,104},{48,112},{56,120},{... | collective-permute-start | bytes 98312 | tf_op jit(solution)/shard_map/ppermute | solution.py:444
  33.5 4.3 %collective-permute-start.3 = (f32[16,512]{1,0:T(8,128)S(1)}, f32[16,512]{1,0:T(8,128)S(1)}, u32[]{:S(2)}, u32[]{:S(2)}) collective-permute-start(f32[16,512]{1,0:T(8,128)S(1)} %get-tuple-element.58), channel_id=1, source_target_pairs={{0,32},{8,40},{16,48},{24,56},{32,64},{40,72},{48,80},{56,88},{64,... | collective-permute-start | bytes 98312 | tf_op jit(solution)/shard_map/ppermute | solution.py:444
  38.2 14.3 %collective-permute-start.14 = (bf16[128,4096]{1,0:T(8,128)(2,1)S(1)}, bf16[128,4096]{1,0:T(8,128)(2,1)S(1)}, u32[]{:S(2)}, u32[]{:S(2)}) collective-permute-start(bf16[128,4096]{1,0:T(8,128)(2,1)S(1)} %collective-permute-done.10.refs_3_), channel_id=1, source_target_pairs={{0,8},{1,9},{2,10},{3,11},{4,12},{5,13},{6,14},{7,15},{8,0},{9,1},... | collective-permute-start | bytes 3145736 | tf_op jit(solution)/shard_map/ppermute | solution.py:286
  38.4 9.3 %collective-permute-start.9 = (bf16[32,4096]{1,0:T(8,128)(2,1)S(1)}, bf16[32,4096]{1,0:T(8,128)(2,1)S(1)}, u32[]{:S(2)}, u32[]{:S(2)}) collective-permute-start(bf16[32,4096]{1,0:T(8,128)(2,1)S(1)} %get-tuple-element.95), channel_id=1, source_target_pairs={{0,96},{1,97},{2,98},{3,99},{4,100},{5,101},{6,102},{7,103},{8,104... | collective-permute-start | bytes 786440 | tf_op jit(solution)/shard_map/ppermute | solution.py:286
  39.5 9.6 %collective-permute-start.8 = (bf16[32,4096]{1,0:T(8,128)(2,1)S(1)}, bf16[32,4096]{1,0:T(8,128)(2,1)S(1)}, u32[]{:S(2)}, u32[]{:S(2)}) collective-permute-start(bf16[32,4096]{1,0:T(8,128)(2,1)S(1)} %get-tuple-element.96), channel_id=1, source_target_pairs={{0,32},{1,33},{2,34},{3,35},{4,36},{5,37},{6,38},{7,39},{8,40},{9,... | collective-permute-start | bytes 786440 | tf_op jit(solution)/shard_map/ppermute | solution.py:286
  40.9 11.7 %collective-permute-start.11 = (bf16[64,4096]{1,0:T(8,128)(2,1)S(1)}, bf16[64,4096]{1,0:T(8,128)(2,1)S(1)}, u32[]{:S(2)}, u32[]{:S(2)}) collective-permute-start(bf16[64,4096]{1,0:T(8,128)(2,1)S(1)} %collective-permute-done.7.refs_0_), channel_id=1, source_target_pairs={{0,8},{1,9},{2,10},{3,11},{4,12},{5,13},{6,14},{7,15},{8,0},{9,1},... | collective-permute-start | bytes 1572872 | tf_op jit(solution)/shard_map/ppermute | solution.py:286
  47.7 1.6 %collective-permute-start.13 = (bf16[32,4096]{1,0:T(8,128)(2,1)S(1)}, bf16[32,4096]{1,0:T(8,128)(2,1)S(1)}, u32[]{:S(2)}, u32[]{:S(2)}) collective-permute-start(bf16[32,4096]{1,0:T(8,128)(2,1)S(1)} %collective-permute-done.9.refs_2_), channel_id=1, source_target_pairs={{0,8},{1,9},{2,10},{3,11},{4,12},{5,13},{6,14},{7,15},{8,0},{9,1},... | collective-permute-start | bytes 786440 | tf_op jit(solution)/shard_map/ppermute | solution.py:286
  49.1 2.0 %collective-permute-start.12 = (bf16[32,4096]{1,0:T(8,128)(2,1)S(1)}, bf16[32,4096]{1,0:T(8,128)(2,1)S(1)}, u32[]{:S(2)}, u32[]{:S(2)}) collective-permute-start(bf16[32,4096]{1,0:T(8,128)(2,1)S(1)} %collective-permute-done.8.refs_1_), channel_id=1, source_target_pairs={{0,8},{1,9},{2,10},{3,11},{4,12},{5,13},{6,14},{7,15},{8,0},{9,1},... | collective-permute-start | bytes 786440 | tf_op jit(solution)/shard_map/ppermute | solution.py:286
  49.1 16.6 %collective-permute-start.15 = (bf16[256,512]{1,0:T(8,128)(2,1)S(1)}, bf16[256,512]{1,0:T(8,128)(2,1)S(1)}, u32[]{:S(2)}, u32[]{:S(2)}) collective-permute-start(bf16[256,512]{1,0:T(8,128)(2,1)S(1)} %get-tuple-element.66), channel_id=1, source_target_pairs={{0,4},{1,5},{2,6},{3,7},{4,0},{5,1},{6,2},{7,3},{8,12},{9,13},{10,... | collective-permute-start | bytes 786440 | tf_op jit(solution)/shard_map/ppermute | solution.py:286
  49.4 11.8 %collective-permute-start.6 = (bf16[128,512]{1,0:T(8,128)(2,1)S(1)}, bf16[128,512]{1,0:T(8,128)(2,1)S(1)}, u32[]{:S(2)}, u32[]{:S(2)}) collective-permute-start(bf16[128,512]{1,0:T(8,128)(2,1)S(1)} %get-tuple-element.63), channel_id=1, source_target_pairs={{0,4},{1,5},{2,6},{3,7},{4,0},{5,1},{6,2},{7,3},{8,12},{9,13},{10,... | collective-permute-start | bytes 393224 | tf_op jit(solution)/shard_map/ppermute | solution.py:286
  51.2 17.1 %collective-permute-start.16 = (bf16[128,512]{1,0:T(8,128)(2,1)S(1)}, bf16[128,512]{1,0:T(8,128)(2,1)S(1)}, u32[]{:S(2)}, u32[]{:S(2)}) collective-permute-start(bf16[128,512]{1,0:T(8,128)(2,1)S(1)} %get-tuple-element.67), channel_id=1, source_target_pairs={{0,4},{1,5},{2,6},{3,7},{4,0},{5,1},{6,2},{7,3},{8,12},{9,13},{10,... | collective-permute-start | bytes 393224 | tf_op jit(solution)/shard_map/ppermute | solution.py:286
  52.5 8.6 %copy-start = (bf16[512,4096]{1,0:T(8,128)(2,1)S(1)}, bf16[512,4096]{1,0:T(8,128)(2,1)}, u32[]{:S(2)}) copy-start(bf16[512,4096]{1,0:T(8,128)(2,1)} %refs_2_.11) | copy-start | bytes 12582916
  61.9 13.0 %collective-permute-start.20 = (bf16[128,512]{1,0:T(8,128)(2,1)S(1)}, bf16[128,512]{1,0:T(8,128)(2,1)S(1)}, u32[]{:S(2)}, u32[]{:S(2)}) collective-permute-start(bf16[128,512]{1,0:T(8,128)(2,1)S(1)} %get-tuple-element.80), channel_id=1, source_target_pairs={{0,1},{1,2},{2,3},{3,0},{4,5},{5,6},{6,7},{7,4},{8,9},{9,10},{10,1... | collective-permute-start | bytes 393224 | tf_op jit(solution)/shard_map/ppermute | solution.py:286
  63.9 42.7 %collective-permute-start.17 = (bf16[128,512]{1,0:T(8,128)(2,1)S(1)}, bf16[128,512]{1,0:T(8,128)(2,1)S(1)}, u32[]{:S(2)}, u32[]{:S(2)}) collective-permute-start(bf16[128,512]{1,0:T(8,128)(2,1)S(1)} %get-tuple-element.70), channel_id=1, source_target_pairs={{0,1},{1,2},{2,3},{3,0},{4,5},{5,6},{6,7},{7,4},{8,9},{9,10},{10,1... | collective-permute-start | bytes 393224 | tf_op jit(solution)/shard_map/ppermute | solution.py:286
  69.8 6.4 %collective-permute-start.18 = (bf16[128,512]{1,0:T(8,128)(2,1)S(1)}, bf16[128,512]{1,0:T(8,128)(2,1)S(1)}, u32[]{:S(2)}, u32[]{:S(2)}) collective-permute-start(bf16[128,512]{1,0:T(8,128)(2,1)S(1)} %get-tuple-element.77), channel_id=1, source_target_pairs={{0,3},{1,0},{2,1},{3,2},{4,7},{5,4},{6,5},{7,6},{8,11},{9,8},{10,9... | collective-permute-start | bytes 393224 | tf_op jit(solution)/shard_map/ppermute | solution.py:286
  71.2 22.9 %collective-permute-start.22 = (bf16[128,512]{1,0:T(8,128)(2,1)S(1)}, bf16[128,512]{1,0:T(8,128)(2,1)S(1)}, u32[]{:S(2)}, u32[]{:S(2)}) collective-permute-start(bf16[128,512]{1,0:T(8,128)(2,1)S(1)} %get-tuple-element.81), channel_id=1, source_target_pairs={{0,3},{1,0},{2,1},{3,2},{4,7},{5,4},{6,5},{7,6},{8,11},{9,8},{10,9... | collective-permute-start | bytes 393224 | tf_op jit(solution)/shard_map/ppermute | solution.py:286
  72.4 21.2 %collective-permute-start.25 = (bf16[256,512]{1,0:T(8,128)(2,1)S(1)}, bf16[256,512]{1,0:T(8,128)(2,1)S(1)}, u32[]{:S(2)}, u32[]{:S(2)}) collective-permute-start(bf16[256,512]{1,0:T(8,128)(2,1)S(1)} %get-tuple-element.83), channel_id=1, source_target_pairs={{0,3},{1,0},{2,1},{3,2},{4,7},{5,4},{6,5},{7,6},{8,11},{9,8},{10,9... | collective-permute-start | bytes 786440 | tf_op jit(solution)/shard_map/ppermute | solution.py:286
  74.9 18.2 %collective-permute-start.27 = (bf16[256,512]{1,0:T(8,128)(2,1)S(1)}, bf16[256,512]{1,0:T(8,128)(2,1)S(1)}, u32[]{:S(2)}, u32[]{:S(2)}) collective-permute-start(bf16[256,512]{1,0:T(8,128)(2,1)S(1)} %get-tuple-element.86), channel_id=1, source_target_pairs={{0,1},{1,2},{2,3},{3,0},{4,5},{5,6},{6,7},{7,4},{8,9},{9,10},{10,1... | collective-permute-start | bytes 786440 | tf_op jit(solution)/shard_map/ppermute | solution.py:286
  76.3 8.9 %collective-permute-start.32 = (bf16[128,512]{1,0:T(8,128)(2,1)S(1)}, bf16[128,512]{1,0:T(8,128)(2,1)S(1)}, u32[]{:S(2)}, u32[]{:S(2)}) collective-permute-start(bf16[128,512]{1,0:T(8,128)(2,1)S(1)} %get-tuple-element.90), channel_id=1, source_target_pairs={{0,3},{1,0},{2,1},{3,2},{4,7},{5,4},{6,5},{7,6},{8,11},{9,8},{10,9... | collective-permute-start | bytes 393224 | tf_op jit(solution)/shard_map/ppermute | solution.py:286
  85.2 6.2 %collective-permute-start.34 = (bf16[128,512]{1,0:T(8,128)(2,1)S(1)}, bf16[128,512]{1,0:T(8,128)(2,1)S(1)}, u32[]{:S(2)}, u32[]{:S(2)}) collective-permute-start(bf16[128,512]{1,0:T(8,128)(2,1)S(1)} %get-tuple-element.93), channel_id=1, source_target_pairs={{0,1},{1,2},{2,3},{3,0},{4,5},{5,6},{6,7},{7,4},{8,9},{9,10},{10,1... | collective-permute-start | bytes 393224 | tf_op jit(solution)/shard_map/ppermute | solution.py:286
  91.3 9.5 %collective-permute-start.29 = (bf16[256,512]{1,0:T(8,128)(2,1)S(1)}, bf16[256,512]{1,0:T(8,128)(2,1)S(1)}, u32[]{:S(2)}, u32[]{:S(2)}) collective-permute-start(bf16[256,512]{1,0:T(8,128)(2,1)S(1)} %get-tuple-element.87), channel_id=1, source_target_pairs={{0,3},{1,0},{2,1},{3,2},{4,7},{5,4},{6,5},{7,6},{8,11},{9,8},{10,9... | collective-permute-start | bytes 786440 | tf_op jit(solution)/shard_map/ppermute | solution.py:286
  93.1 7.7 %collective-permute-start.21 = (bf16[128,512]{1,0:T(8,128)(2,1)S(1)}, bf16[128,512]{1,0:T(8,128)(2,1)S(1)}, u32[]{:S(2)}, u32[]{:S(2)}) collective-permute-start(bf16[128,512]{1,0:T(8,128)(2,1)S(1)} %add_convert_fusion.7), channel_id=1, source_target_pairs={{0,1},{1,2},{2,3},{3,0},{4,5},{5,6},{6,7},{7,4},{8,9},{9,10},{10,1... | collective-permute-start | bytes 393224 | tf_op jit(solution)/shard_map/ppermute | solution.py:286
  93.6 12.8 %collective-permute-start.28 = (bf16[256,512]{1,0:T(8,128)(2,1)S(1)}, bf16[256,512]{1,0:T(8,128)(2,1)S(1)}, u32[]{:S(2)}, u32[]{:S(2)}) collective-permute-start(bf16[256,512]{1,0:T(8,128)(2,1)S(1)} %add_convert_fusion.1), channel_id=1, source_target_pairs={{0,1},{1,2},{2,3},{3,0},{4,5},{5,6},{6,7},{7,4},{8,9},{9,10},{10,1... | collective-permute-start | bytes 786440 | tf_op jit(solution)/shard_map/ppermute | solution.py:286
  94.1 19.6 %collective-permute-start.24 = (bf16[256,512]{1,0:T(8,128)(2,1)S(1)}, bf16[256,512]{1,0:T(8,128)(2,1)S(1)}, u32[]{:S(2)}, u32[]{:S(2)}) collective-permute-start(bf16[256,512]{1,0:T(8,128)(2,1)S(1)} %get-tuple-element.73), channel_id=1, source_target_pairs={{0,1},{1,2},{2,3},{3,0},{4,5},{5,6},{6,7},{7,4},{8,9},{9,10},{10,1... | collective-permute-start | bytes 786440 | tf_op jit(solution)/shard_map/ppermute | solution.py:286
  100.8 12.3 %collective-permute-start.31 = (bf16[128,512]{1,0:T(8,128)(2,1)S(1)}, bf16[128,512]{1,0:T(8,128)(2,1)S(1)}, u32[]{:S(2)}, u32[]{:S(2)}) collective-permute-start(bf16[128,512]{1,0:T(8,128)(2,1)S(1)} %get-tuple-element.88), channel_id=1, source_target_pairs={{0,1},{1,2},{2,3},{3,0},{4,5},{5,6},{6,7},{7,4},{8,9},{9,10},{10,1... | collective-permute-start | bytes 393224 | tf_op jit(solution)/shard_map/ppermute | solution.py:286
  100.9 9.0 %collective-permute-start.36 = (bf16[128,512]{1,0:T(8,128)(2,1)S(1)}, bf16[128,512]{1,0:T(8,128)(2,1)S(1)}, u32[]{:S(2)}, u32[]{:S(2)}) collective-permute-start(bf16[128,512]{1,0:T(8,128)(2,1)S(1)} %get-tuple-element.94), channel_id=1, source_target_pairs={{0,3},{1,0},{2,1},{3,2},{4,7},{5,4},{6,5},{7,6},{8,11},{9,8},{10,9... | collective-permute-start | bytes 393224 | tf_op jit(solution)/shard_map/ppermute | solution.py:286
  106.4 6.2 %collective-permute-start.35 = (bf16[128,512]{1,0:T(8,128)(2,1)S(1)}, bf16[128,512]{1,0:T(8,128)(2,1)S(1)}, u32[]{:S(2)}, u32[]{:S(2)}) collective-permute-start(bf16[128,512]{1,0:T(8,128)(2,1)S(1)} %add_convert_fusion.4), channel_id=1, source_target_pairs={{0,1},{1,2},{2,3},{3,0},{4,5},{5,6},{6,7},{7,4},{8,9},{9,10},{10,1... | collective-permute-start | bytes 393224 | tf_op jit(solution)/shard_map/ppermute | solution.py:286
  106.5 8.7 %collective-permute-start.19 = (bf16[128,512]{1,0:T(8,128)(2,1)S(1)}, bf16[128,512]{1,0:T(8,128)(2,1)S(1)}, u32[]{:S(2)}, u32[]{:S(2)}) collective-permute-start(bf16[128,512]{1,0:T(8,128)(2,1)S(1)} %add_convert_fusion.8), channel_id=1, source_target_pairs={{0,3},{1,0},{2,1},{3,2},{4,7},{5,4},{6,5},{7,6},{8,11},{9,8},{10,9... | collective-permute-start | bytes 393224 | tf_op jit(solution)/shard_map/ppermute | solution.py:286
  109.8 11.9 %collective-permute-start.26 = (bf16[256,512]{1,0:T(8,128)(2,1)S(1)}, bf16[256,512]{1,0:T(8,128)(2,1)S(1)}, u32[]{:S(2)}, u32[]{:S(2)}) collective-permute-start(bf16[256,512]{1,0:T(8,128)(2,1)S(1)} %add_convert_fusion.2), channel_id=1, source_target_pairs={{0,3},{1,0},{2,1},{3,2},{4,7},{5,4},{6,5},{7,6},{8,11},{9,8},{10,9... | collective-permute-start | bytes 786440 | tf_op jit(solution)/shard_map/ppermute | solution.py:286
  112.6 9.2 %collective-permute-start.30 = (bf16[256,512]{1,0:T(8,128)(2,1)S(1)}, bf16[256,512]{1,0:T(8,128)(2,1)S(1)}, u32[]{:S(2)}, u32[]{:S(2)}) collective-permute-start(bf16[256,512]{1,0:T(8,128)(2,1)S(1)} %add_convert_fusion), channel_id=1, source_target_pairs={{0,4},{1,5},{2,6},{3,7},{4,0},{5,1},{6,2},{7,3},{8,12},{9,13},{10,... | collective-permute-start | bytes 786440 | tf_op jit(solution)/shard_map/ppermute | solution.py:286
  113.1 5.0 %collective-permute-start.33 = (bf16[128,512]{1,0:T(8,128)(2,1)S(1)}, bf16[128,512]{1,0:T(8,128)(2,1)S(1)}, u32[]{:S(2)}, u32[]{:S(2)}) collective-permute-start(bf16[128,512]{1,0:T(8,128)(2,1)S(1)} %add_convert_fusion.5), channel_id=1, source_target_pairs={{0,3},{1,0},{2,1},{3,2},{4,7},{5,4},{6,5},{7,6},{8,11},{9,8},{10,9... | collective-permute-start | bytes 393224 | tf_op jit(solution)/shard_map/ppermute | solution.py:286
  113.7 6.7 %collective-permute-start.23 = (bf16[128,512]{1,0:T(8,128)(2,1)S(1)}, bf16[128,512]{1,0:T(8,128)(2,1)S(1)}, u32[]{:S(2)}, u32[]{:S(2)}) collective-permute-start(bf16[128,512]{1,0:T(8,128)(2,1)S(1)} %add_convert_fusion.6), channel_id=1, source_target_pairs={{0,4},{1,5},{2,6},{3,7},{4,0},{5,1},{6,2},{7,3},{8,12},{9,13},{10,... | collective-permute-start | bytes 393224 | tf_op jit(solution)/shard_map/ppermute | solution.py:286
  115.2 6.5 %collective-permute-start.37 = (bf16[128,512]{1,0:T(8,128)(2,1)S(1)}, bf16[128,512]{1,0:T(8,128)(2,1)S(1)}, u32[]{:S(2)}, u32[]{:S(2)}) collective-permute-start(bf16[128,512]{1,0:T(8,128)(2,1)S(1)} %add_convert_fusion.3), channel_id=1, source_target_pairs={{0,4},{1,5},{2,6},{3,7},{4,0},{5,1},{6,2},{7,3},{8,12},{9,13},{10,... | collective-permute-start | bytes 393224 | tf_op jit(solution)/shard_map/ppermute | solution.py:286
where the time goes:
time: 123 us
  waiting for transfers between devices  61.6 us (50%)
  starting transfers between devices  46.1 us (37%)
  Pallas kernels  14.4 us (12%)
    ppermute x32, waiting for transfers between devices, move(): return lax.ppermute(array, ('ctx', 'tp'), route(change))  44.5 us
    ppermute x32, starting transfers between devices, move(): return lax.ppermute(array, ('ctx', 'tp'), route(change))  33.4 us
    ppermute x3, waiting for transfers between devices, layer(): near.append(lax.ppermute(last, 'ctx', pairs))  16.4 us
    pallas_call x12, Pallas kernels, call(): pl.pallas_call(kernel, out_shape=out_shape, in_specs=[vmem()] * len(args)...  11.2 us
    ppermute x3, starting transfers between devices, layer(): lax.ppermute(total, 'ctx', [(c, c + 4 * k) for c in range(16 - 4 * k)])  8.98 us
    ppermute x3, starting transfers between devices, layer(): near.append(lax.ppermute(last, 'ctx', pairs))  3.72 us
    pallas_call x1, Pallas kernels, cut_slabs(): pl.pallas_call(slab_kernel, out_shape=[jax.ShapeDtypeStruct((rows, w_out....  2.72 us
  transfers between devices with their start and end apart: 38, of which 15 were waited for; matrix products, arithmetic and copies ran while one was open for 0% of the time, Pallas kernels for 9%

commit v1 on v0

--- a/solution.py
+++ b/solution.py
@@ -384,19 +384,33 @@
 
 
 def finish_kernel(*refs):
-    out_ref = refs[-1]
+    inputs, (out_ref, total_ref, sems) = refs[:-3], refs[-3:]
     near = lax.axis_index("tp") // 4
+    count = len(PARTS)
+    copies = []
     start = 0
     for part, rows in enumerate(PARTS):
-        own = refs[part]
-        right, left, swapped = refs[len(PARTS) + part * 3 : len(PARTS) + part * 3 + 3]
+        swapped = inputs[count + part * 3 + 2]
+        there = pl.multiple_of((1 - near) * sum(PARTS) + start, CHUNK)
+        copies.append(
+            pltpu.make_async_copy(swapped, out_ref.at[pl.ds(there, rows)], sems.at[part, 0])
+        )
+        copies[-1].start()
+        start += rows
+    start = 0
+    for part, rows in enumerate(PARTS):
+        own, (right, left) = inputs[part], inputs[count + part * 3 : count + part * 3 + 2]
         total = own[...].astype(jnp.float32) + right[...].astype(jnp.float32)
-        total = (total + left[...].astype(jnp.float32)).astype(jnp.bfloat16)
+        mine = total_ref.at[start : start + rows]
+        mine[...] = (total + left[...].astype(jnp.float32)).astype(jnp.bfloat16)
         here = pl.multiple_of(near * sum(PARTS) + start, CHUNK)
-        there = pl.multiple_of((1 - near) * sum(PARTS) + start, CHUNK)
-        out_ref[pl.ds(here, rows), :] = total
-        out_ref[pl.ds(there, rows), :] = swapped[...]
+        copies.append(
+            pltpu.make_async_copy(mine, out_ref.at[pl.ds(here, rows)], sems.at[part, 1])
+        )
+        copies[-1].start()
         start += rows
+    for copy in copies:
+        copy.wait()
 
 
 def plus(*arrays):
@@ -488,7 +502,18 @@
         left_o = move(plus(left_o, far_o), along("z", 4, -1))
         swapped = move(plus(own_p, right_p, left_p), along("near", 2, 1))
         rest += [right_o, left_o, swapped]
-    return call(finish_kernel, 1, shape((length, 512), jnp.bfloat16), *finals, *rest)
+    return pl.pallas_call(
+        finish_kernel,
+        out_shape=shape((length, 512), jnp.bfloat16),
+        in_specs=[vmem()] * (len(finals) + len(rest)),
+        out_specs=anywhere(),
+        scratch_shapes=[
+            pltpu.VMEM((sum(PARTS), 512), jnp.bfloat16),
+            pltpu.SemaphoreType.DMA((len(PARTS), 2)),
+        ],
+        cost_estimate=cost(1),
+        compiler_params=pltpu.CompilerParams(vmem_limit_bytes=LIMIT),
+    )(*finals, *rest)
 
 
 def solution(mesh):

time: 123 us -> 123 us (level)
    pallas_call x12 -> x11, Pallas kernels: 11.2 us -> 10.1 us  [call(): pl.pallas_call(kernel, out_shape=out_shape, in_specs=[vmem()] * len(args)...]
where the time goes in v1:
time: 123 us
  waiting for transfers between devices  61.6 us (50%)
  starting transfers between devices  46.1 us (37%)
  Pallas kernels  14.2 us (12%)
    ppermute x32, waiting for transfers between devices, move(): return lax.ppermute(array, ('ctx', 'tp'), route(change))  44.5 us
    ppermute x32, starting transfers between devices, move(): return lax.ppermute(array, ('ctx', 'tp'), route(change))  33.4 us
    ppermute x3, waiting for transfers between devices, layer(): near.append(lax.ppermute(last, 'ctx', pairs))  16.4 us
    pallas_call x11, Pallas kernels, call(): pl.pallas_call(kernel, out_shape=out_shape, in_specs=[vmem()] * len(args)...  10.1 us
    ppermute x3, starting transfers between devices, layer(): lax.ppermute(total, 'ctx', [(c, c + 4 * k) for c in range(16 - 4 * k)])  8.98 us
    ppermute x3, starting transfers between devices, layer(): near.append(lax.ppermute(last, 'ctx', pairs))  3.72 us
    pallas_call x1, Pallas kernels, cut_slabs(): pl.pallas_call(slab_kernel, out_shape=[jax.ShapeDtypeStruct((rows, w_out....  2.72 us
  transfers between devices with their start and end apart: 38, of which 15 were waited for; matrix products, arithmetic and copies ran while one was open for 0% of the time, Pallas kernels for 9%

profile of v1, /device:TPU:0, one launch (start us, length us, event | category | flops | bytes accessed | tf_op | source)
XLA Modules:
  0.0 123.0 jit_solution(1428242036157735351)
XLA Ops:
  0.0 2.7 %shard_map.69 = (bf16[64,4096]{1,0:T(8,128)(2,1)}, bf16[128,4096]{1,0:T(8,128)(2,1)}) custom-call(bf16[512,4096]{1,0:T(8,128)(2,1)} %refs_2_.11), custom_call_target="tpu_custom_call" | custom-call | bytes 3000000 | tf_op jit(solution)/shard_map/pallas_call | solution.py:322
  2.7 1.7 %collective-permute-start.10 = (bf16[128,4096]{1,0:T(8,128)(2,1)}, bf16[128,4096]{1,0:T(8,128)(2,1)S(1)}, u32[]{:S(2)}, u32[]{:S(2)}) collective-permute-start(bf16[128,4096]{1,0:T(8,128)(2,1)} %get-tuple-element.65), channel_id=1, source_target_pairs={{0,4},{1,5},{2,6},{3,7},{4,0},{5,1},{6,2},{7,3},{8,28},{9,29},{10,... | collective-permute-start | bytes 3145736 | tf_op jit(solution)/shard_map/ppermute | solution.py:286
  4.9 2.1 %shard_map.64 = (f32[128,512]{1,0:T(8,128)S(1)}, f32[16,512]{1,0:T(8,128)S(1)}, f32[16,512]{1,0:T(8,128)S(1)}, bf16[128,512]{1,0:T(8,128)(2,1)S(1)}, bf16[4096,1...) custom-call(f32[32,256]{1,0:T(8,128)S(1)} %pad_maximum_fusion.modes_ref, bf16[1024,512]{1,0:T(8,128)(2,1)S(1)} %copy-done.2, ...), custom_call_target="tpu_custom_call" | custom-call | bytes 9000000 | tf_op jit(solution)/shard_map/pallas_call | solution.py:263
  7.0 2.1 %collective-permute-start.2 = (f32[16,512]{1,0:T(8,128)S(1)}, f32[16,512]{1,0:T(8,128)S(1)}, u32[]{:S(2)}, u32[]{:S(2)}) collective-permute-start(f32[16,512]{1,0:T(8,128)S(1)} %get-tuple-element.51.last_ref), channel_id=1, source_target_pairs={{0,24},{8,16},{16,8},{24,0},{32,56},{40,48},{48,40},{56,32},{64,88... | collective-permute-start | bytes 98312 | tf_op jit(solution)/shard_map/ppermute | solution.py:455
  9.1 1.6 %collective-permute-start.1 = (f32[16,512]{1,0:T(8,128)S(1)}, f32[16,512]{1,0:T(8,128)S(1)}, u32[]{:S(2)}, u32[]{:S(2)}) collective-permute-start(f32[16,512]{1,0:T(8,128)S(1)} %get-tuple-element.51.last_ref), channel_id=1, source_target_pairs={{0,16},{8,24},{16,0},{24,8},{32,48},{40,56},{48,32},{56,40},{64,80... | collective-permute-start | bytes 98312 | tf_op jit(solution)/shard_map/ppermute | solution.py:455
  10.7 12.9 %collective-permute-done.2.three_ref = f32[16,512]{1,0:T(8,128)S(1)} collective-permute-done((f32[16,512]{1,0:T(8,128)S(1)}, f32[16,512]{1,0:T(8,128)S(1)}, u32[]{:S(2)}, u32[]{:S(2)}) %collective-permute-start.2) | collective-permute-done | bytes 32800 | tf_op jit(solution)/shard_map/ppermute | solution.py:455
  23.6 3.5 %collective-permute-done.1.two_ref = f32[16,512]{1,0:T(8,128)S(1)} collective-permute-done((f32[16,512]{1,0:T(8,128)S(1)}, f32[16,512]{1,0:T(8,128)S(1)}, u32[]{:S(2)}, u32[]{:S(2)}) %collective-permute-start.1) | collective-permute-done | bytes 32800 | tf_op jit(solution)/shard_map/ppermute | solution.py:455
  27.2 4.9 %collective-permute-start.5 = (f32[16,512]{1,0:T(8,128)S(1)}, f32[16,512]{1,0:T(8,128)S(1)}, u32[]{:S(2)}, u32[]{:S(2)}) collective-permute-start(f32[16,512]{1,0:T(8,128)S(1)} %get-tuple-element.58), channel_id=1, source_target_pairs={{0,96},{8,104},{16,112},{24,120},{1,97},{9,105},{17,113},{25,121},... | collective-permute-start | bytes 98312 | tf_op jit(solution)/shard_map/ppermute | solution.py:458
  32.2 1.3 %collective-permute-start.4 = (f32[16,512]{1,0:T(8,128)S(1)}, f32[16,512]{1,0:T(8,128)S(1)}, u32[]{:S(2)}, u32[]{:S(2)}) collective-permute-start(f32[16,512]{1,0:T(8,128)S(1)} %get-tuple-element.58), channel_id=1, source_target_pairs={{0,64},{8,72},{16,80},{24,88},{32,96},{40,104},{48,112},{56,120},{... | collective-permute-start | bytes 98312 | tf_op jit(solution)/shard_map/ppermute | solution.py:458
  33.5 2.8 %collective-permute-start.3 = (f32[16,512]{1,0:T(8,128)S(1)}, f32[16,512]{1,0:T(8,128)S(1)}, u32[]{:S(2)}, u32[]{:S(2)}) collective-permute-start(f32[16,512]{1,0:T(8,128)S(1)} %get-tuple-element.58), channel_id=1, source_target_pairs={{0,32},{8,40},{16,48},{24,56},{32,64},{40,72},{48,80},{56,88},{64,... | collective-permute-start | bytes 98312 | tf_op jit(solution)/shard_map/ppermute | solution.py:458
  36.2 0.9 shard_map.66.near_ref
  37.1 0.7 collective-permute-done.3.one_ref
  38.4 1.1 collective-permute-start.9
  39.5 1.3 %collective-permute-start.8 = (bf16[32,4096]{1,0:T(8,128)(2,1)S(1)}, bf16[32,4096]{1,0:T(8,128)(2,1)S(1)}, u32[]{:S(2)}, u32[]{:S(2)}) collective-permute-start(bf16[32,4096]{1,0:T(8,128)(2,1)S(1)} %get-tuple-element.96), channel_id=1, source_target_pairs={{0,32},{1,33},{2,34},{3,35},{4,36},{5,37},{6,38},{7,39},{8,40},{9,... | collective-permute-start | bytes 786440 | tf_op jit(solution)/shard_map/ppermute | solution.py:286
  41.1 6.7 %collective-permute-done.9.refs_2_ = bf16[32,4096]{1,0:T(8,128)(2,1)S(1)} collective-permute-done((bf16[32,4096]{1,0:T(8,128)(2,1)S(1)}, bf16[32,4096]{1,0:T(8,128)(2,1)S(1)}, u32[]{:S(2)}, u32[]{:S(2)}) %collective-permute-start.9) | collective-permute-done | bytes 262176 | tf_op jit(solution)/shard_map/ppermute | solution.py:286
  47.7 1.4 %collective-permute-done.8.refs_1_ = bf16[32,4096]{1,0:T(8,128)(2,1)S(1)} collective-permute-done((bf16[32,4096]{1,0:T(8,128)(2,1)S(1)}, bf16[32,4096]{1,0:T(8,128)(2,1)S(1)}, u32[]{:S(2)}, u32[]{:S(2)}) %collective-permute-start.8) | collective-permute-done | bytes 262176 | tf_op jit(solution)/shard_map/ppermute | solution.py:286
  49.4 1.8 %collective-permute-start.6 = (bf16[128,512]{1,0:T(8,128)(2,1)S(1)}, bf16[128,512]{1,0:T(8,128)(2,1)S(1)}, u32[]{:S(2)}, u32[]{:S(2)}) collective-permute-start(bf16[128,512]{1,0:T(8,128)(2,1)S(1)} %get-tuple-element.63), channel_id=1, source_target_pairs={{0,4},{1,5},{2,6},{3,7},{4,0},{5,1},{6,2},{7,3},{8,12},{9,13},{10,... | collective-permute-start | bytes 393224 | tf_op jit(solution)/shard_map/ppermute | solution.py:286
  51.4 1.1 shard_map.67.refs_0_
  53.0 8.1 %collective-permute-done.6.refs_1_ = bf16[128,512]{1,0:T(8,128)(2,1)S(1)} collective-permute-done((bf16[128,512]{1,0:T(8,128)(2,1)S(1)}, bf16[128,512]{1,0:T(8,128)(2,1)S(1)}, u32[]{:S(2)}, u32[]{:S(2)}) %collective-permute-start.6) | collective-permute-done | bytes 131104 | tf_op jit(solution)/shard_map/ppermute | solution.py:286
  61.1 0.7 shard_map.72
  61.9 2.0 %collective-permute-start.20 = (bf16[128,512]{1,0:T(8,128)(2,1)S(1)}, bf16[128,512]{1,0:T(8,128)(2,1)S(1)}, u32[]{:S(2)}, u32[]{:S(2)}) collective-permute-start(bf16[128,512]{1,0:T(8,128)(2,1)S(1)} %get-tuple-element.80), channel_id=1, source_target_pairs={{0,1},{1,2},{2,3},{3,0},{4,5},{5,6},{6,7},{7,4},{8,9},{9,10},{10,1... | collective-permute-start | bytes 393224 | tf_op jit(solution)/shard_map/ppermute | solution.py:286
  63.9 1.9 %collective-permute-start.17 = (bf16[128,512]{1,0:T(8,128)(2,1)S(1)}, bf16[128,512]{1,0:T(8,128)(2,1)S(1)}, u32[]{:S(2)}, u32[]{:S(2)}) collective-permute-start(bf16[128,512]{1,0:T(8,128)(2,1)S(1)} %get-tuple-element.70), channel_id=1, source_target_pairs={{0,1},{1,2},{2,3},{3,0},{4,5},{5,6},{6,7},{7,4},{8,9},{9,10},{10,1... | collective-permute-start | bytes 393224 | tf_op jit(solution)/shard_map/ppermute | solution.py:286
  65.8 0.7 shard_map.75
  66.5 1.8 %shard_map.73 = (bf16[256,512]{1,0:T(8,128)(2,1)S(1)}, bf16[256,512]{1,0:T(8,128)(2,1)S(1)}, bf16[256,512]{1,0:T(8,128)(2,1)S(1)}, bf16[256,512]{1,0:T(8,128)(2,...) custom-call(bf16[512,512]{1,0:T(8,128)(2,1)S(1)} %shard_map.67.refs_0_, ...), custom_call_target="tpu_custom_call" | custom-call | bytes 18000000 | tf_op jit(solution)/shard_map/pallas_call | solution.py:263
  68.8 1.0 shard_map.74
  69.8 1.4 %collective-permute-start.18 = (bf16[128,512]{1,0:T(8,128)(2,1)S(1)}, bf16[128,512]{1,0:T(8,128)(2,1)S(1)}, u32[]{:S(2)}, u32[]{:S(2)}) collective-permute-start(bf16[128,512]{1,0:T(8,128)(2,1)S(1)} %get-tuple-element.77), channel_id=1, source_target_pairs={{0,3},{1,0},{2,1},{3,2},{4,7},{5,4},{6,5},{7,6},{8,11},{9,8},{10,9... | collective-permute-start | bytes 393224 | tf_op jit(solution)/shard_map/ppermute | solution.py:286
  71.2 1.2 collective-permute-start.22
  72.4 1.8 %collective-permute-start.25 = (bf16[256,512]{1,0:T(8,128)(2,1)S(1)}, bf16[256,512]{1,0:T(8,128)(2,1)S(1)}, u32[]{:S(2)}, u32[]{:S(2)}) collective-permute-start(bf16[256,512]{1,0:T(8,128)(2,1)S(1)} %get-tuple-element.83), channel_id=1, source_target_pairs={{0,3},{1,0},{2,1},{3,2},{4,7},{5,4},{6,5},{7,6},{8,11},{9,8},{10,9... | collective-permute-start | bytes 786440 | tf_op jit(solution)/shard_map/ppermute | solution.py:286
  74.1 0.7 shard_map.71
  75.3 1.0 collective-permute-done.18
  76.3 2.5 %collective-permute-start.32 = (bf16[128,512]{1,0:T(8,128)(2,1)S(1)}, bf16[128,512]{1,0:T(8,128)(2,1)S(1)}, u32[]{:S(2)}, u32[]{:S(2)}) collective-permute-start(bf16[128,512]{1,0:T(8,128)(2,1)S(1)} %get-tuple-element.90), channel_id=1, source_target_pairs={{0,3},{1,0},{2,1},{3,2},{4,7},{5,4},{6,5},{7,6},{8,11},{9,8},{10,9... | collective-permute-start | bytes 393224 | tf_op jit(solution)/shard_map/ppermute | solution.py:286
  78.8 6.3 %collective-permute-done.32 = bf16[128,512]{1,0:T(8,128)(2,1)S(1)} collective-permute-done((bf16[128,512]{1,0:T(8,128)(2,1)S(1)}, bf16[128,512]{1,0:T(8,128)(2,1)S(1)}, u32[]{:S(2)}, u32[]{:S(2)}) %collective-permute-start.32) | collective-permute-done | bytes 131104 | tf_op jit(solution)/shard_map/ppermute | solution.py:286
  85.2 1.6 %collective-permute-start.34 = (bf16[128,512]{1,0:T(8,128)(2,1)S(1)}, bf16[128,512]{1,0:T(8,128)(2,1)S(1)}, u32[]{:S(2)}, u32[]{:S(2)}) collective-permute-start(bf16[128,512]{1,0:T(8,128)(2,1)S(1)} %get-tuple-element.93), channel_id=1, source_target_pairs={{0,1},{1,2},{2,3},{3,0},{4,5},{5,6},{6,7},{7,4},{8,9},{9,10},{10,1... | collective-permute-start | bytes 393224 | tf_op jit(solution)/shard_map/ppermute | solution.py:286
  86.8 4.5 %collective-permute-done.34 = bf16[128,512]{1,0:T(8,128)(2,1)S(1)} collective-permute-done((bf16[128,512]{1,0:T(8,128)(2,1)S(1)}, bf16[128,512]{1,0:T(8,128)(2,1)S(1)}, u32[]{:S(2)}, u32[]{:S(2)}) %collective-permute-start.34) | collective-permute-done | bytes 131104 | tf_op jit(solution)/shard_map/ppermute | solution.py:286
  91.3 1.8 %collective-permute-start.29 = (bf16[256,512]{1,0:T(8,128)(2,1)S(1)}, bf16[256,512]{1,0:T(8,128)(2,1)S(1)}, u32[]{:S(2)}, u32[]{:S(2)}) collective-permute-start(bf16[256,512]{1,0:T(8,128)(2,1)S(1)} %get-tuple-element.87), channel_id=1, source_target_pairs={{0,3},{1,0},{2,1},{3,2},{4,7},{5,4},{6,5},{7,6},{8,11},{9,8},{10,9... | collective-permute-start | bytes 786440 | tf_op jit(solution)/shard_map/ppermute | solution.py:286
  94.1 0.8 collective-permute-start.24
  94.9 5.9 %collective-permute-done.21 = bf16[128,512]{1,0:T(8,128)(2,1)S(1)} collective-permute-done((bf16[128,512]{1,0:T(8,128)(2,1)S(1)}, bf16[128,512]{1,0:T(8,128)(2,1)S(1)}, u32[]{:S(2)}, u32[]{:S(2)}) %collective-permute-start.21) | collective-permute-done | bytes 131104 | tf_op jit(solution)/shard_map/ppermute | solution.py:286
  100.9 3.3 %collective-permute-start.36 = (bf16[128,512]{1,0:T(8,128)(2,1)S(1)}, bf16[128,512]{1,0:T(8,128)(2,1)S(1)}, u32[]{:S(2)}, u32[]{:S(2)}) collective-permute-start(bf16[128,512]{1,0:T(8,128)(2,1)S(1)} %get-tuple-element.94), channel_id=1, source_target_pairs={{0,3},{1,0},{2,1},{3,2},{4,7},{5,4},{6,5},{7,6},{8,11},{9,8},{10,9... | collective-permute-start | bytes 393224 | tf_op jit(solution)/shard_map/ppermute | solution.py:286
  104.2 2.2 %collective-permute-done.28 = bf16[256,512]{1,0:T(8,128)(2,1)S(1)} collective-permute-done((bf16[256,512]{1,0:T(8,128)(2,1)S(1)}, bf16[256,512]{1,0:T(8,128)(2,1)S(1)}, u32[]{:S(2)}, u32[]{:S(2)}) %collective-permute-start.28) | collective-permute-done | bytes 262176 | tf_op jit(solution)/shard_map/ppermute | solution.py:286
  106.5 3.3 %collective-permute-start.19 = (bf16[128,512]{1,0:T(8,128)(2,1)S(1)}, bf16[128,512]{1,0:T(8,128)(2,1)S(1)}, u32[]{:S(2)}, u32[]{:S(2)}) collective-permute-start(bf16[128,512]{1,0:T(8,128)(2,1)S(1)} %add_convert_fusion.8), channel_id=1, source_target_pairs={{0,3},{1,0},{2,1},{3,2},{4,7},{5,4},{6,5},{7,6},{8,11},{9,8},{10,9... | collective-permute-start | bytes 393224 | tf_op jit(solution)/shard_map/ppermute | solution.py:286
  109.8 0.5 collective-permute-start.26
  110.3 2.2 %collective-permute-done.35 = bf16[128,512]{1,0:T(8,128)(2,1)S(1)} collective-permute-done((bf16[128,512]{1,0:T(8,128)(2,1)S(1)}, bf16[128,512]{1,0:T(8,128)(2,1)S(1)}, u32[]{:S(2)}, u32[]{:S(2)}) %collective-permute-start.35) | collective-permute-done | bytes 131104 | tf_op jit(solution)/shard_map/ppermute | solution.py:286
  113.1 0.6 collective-permute-start.33
  113.7 1.6 %collective-permute-start.23 = (bf16[128,512]{1,0:T(8,128)(2,1)S(1)}, bf16[128,512]{1,0:T(8,128)(2,1)S(1)}, u32[]{:S(2)}, u32[]{:S(2)}) collective-permute-start(bf16[128,512]{1,0:T(8,128)(2,1)S(1)} %add_convert_fusion.6), channel_id=1, source_target_pairs={{0,4},{1,5},{2,6},{3,7},{4,0},{5,1},{6,2},{7,3},{8,12},{9,13},{10,... | collective-permute-start | bytes 393224 | tf_op jit(solution)/shard_map/ppermute | solution.py:286
  115.7 2.4 %collective-permute-done.33.refs_10_ = bf16[128,512]{1,0:T(8,128)(2,1)S(1)} collective-permute-done((bf16[128,512]{1,0:T(8,128)(2,1)S(1)}, bf16[128,512]{1,0:T(8,128)(2,1)S(1)}, u32[]{:S(2)}, u32[]{:S(2)}) %collective-permute-start.33) | collective-permute-done | bytes 131104 | tf_op jit(solution)/shard_map/ppermute | solution.py:286
  118.2 2.2 %collective-permute-done.23.refs_5_ = bf16[128,512]{1,0:T(8,128)(2,1)S(1)} collective-permute-done((bf16[128,512]{1,0:T(8,128)(2,1)S(1)}, bf16[128,512]{1,0:T(8,128)(2,1)S(1)}, u32[]{:S(2)}, u32[]{:S(2)}) %collective-permute-start.23) | collective-permute-done | bytes 131104 | tf_op jit(solution)/shard_map/ppermute | solution.py:286
  120.4 1.4 %collective-permute-done.37.refs_11_ = bf16[128,512]{1,0:T(8,128)(2,1)S(1)} collective-permute-done((bf16[128,512]{1,0:T(8,128)(2,1)S(1)}, bf16[128,512]{1,0:T(8,128)(2,1)S(1)}, u32[]{:S(2)}, u32[]{:S(2)}) %collective-permute-start.37) | collective-permute-done | bytes 131104 | tf_op jit(solution)/shard_map/ppermute | solution.py:286
  121.8 1.0 shard_map.77
  (65 shorter events, 5.2 us)
Async XLA Ops:
  0.0 4.8 %copy-start.5 = (f32[256,16]{0,1:T(8,128)S(1)}, f32[256,16]{0,1:T(8,128)}, u32[]{:S(2)}) copy-start(f32[256,16]{0,1:T(8,128)} %param.10) | copy-start | bytes 49156
  0.0 4.8 %copy-start.4 = (f32[256,16]{0,1:T(8,128)S(1)}, f32[256,16]{0,1:T(8,128)}, u32[]{:S(2)}) copy-start(f32[256,16]{0,1:T(8,128)} %param.9) | copy-start | bytes 49156
  0.0 4.9 %copy-start.3 = (bf16[1024,512]{1,0:T(8,128)(2,1)S(1)}, bf16[1024,512]{1,0:T(8,128)(2,1)}, u32[]{:S(2)}) copy-start(bf16[1024,512]{1,0:T(8,128)(2,1)} %values_ref.1) | copy-start | bytes 3145732
  0.0 4.9 %copy-start.2 = (bf16[1024,512]{1,0:T(8,128)(2,1)S(1)}, bf16[1024,512]{1,0:T(8,128)(2,1)}, u32[]{:S(2)}) copy-start(bf16[1024,512]{1,0:T(8,128)(2,1)} %keys_ref.1) | copy-start | bytes 3145732
  0.0 37.8 %copy-start.1 = (bf16[1024,512]{1,0:T(8,128)(2,1)S(1)}, bf16[1024,512]{1,0:T(8,128)(2,1)}, u32[]{:S(2)}) copy-start(bf16[1024,512]{1,0:T(8,128)(2,1)} %query_ref.3) | copy-start | bytes 3145732
  2.7 35.5 %collective-permute-start.10 = (bf16[128,4096]{1,0:T(8,128)(2,1)}, bf16[128,4096]{1,0:T(8,128)(2,1)S(1)}, u32[]{:S(2)}, u32[]{:S(2)}) collective-permute-start(bf16[128,4096]{1,0:T(8,128)(2,1)} %get-tuple-element.65), channel_id=1, source_target_pairs={{0,4},{1,5},{2,6},{3,7},{4,0},{5,1},{6,2},{7,3},{8,28},{9,29},{10,... | collective-permute-start | bytes 3145736 | tf_op jit(solution)/shard_map/ppermute | solution.py:286
  4.4 33.9 %collective-permute-start.7 = (bf16[64,4096]{1,0:T(8,128)(2,1)}, bf16[64,4096]{1,0:T(8,128)(2,1)S(1)}, u32[]{:S(2)}, u32[]{:S(2)}) collective-permute-start(bf16[64,4096]{1,0:T(8,128)(2,1)} %get-tuple-element.64), channel_id=1, source_target_pairs={{0,4},{1,5},{2,6},{3,7},{4,0},{5,1},{6,2},{7,3},{8,28},{9,29},{10,... | collective-permute-start | bytes 1572872 | tf_op jit(solution)/shard_map/ppermute | solution.py:286
  7.0 16.6 %collective-permute-start.2 = (f32[16,512]{1,0:T(8,128)S(1)}, f32[16,512]{1,0:T(8,128)S(1)}, u32[]{:S(2)}, u32[]{:S(2)}) collective-permute-start(f32[16,512]{1,0:T(8,128)S(1)} %get-tuple-element.51.last_ref), channel_id=1, source_target_pairs={{0,24},{8,16},{16,8},{24,0},{32,56},{40,48},{48,40},{56,32},{64,88... | collective-permute-start | bytes 98312 | tf_op jit(solution)/shard_map/ppermute | solution.py:455
  9.1 18.0 %collective-permute-start.1 = (f32[16,512]{1,0:T(8,128)S(1)}, f32[16,512]{1,0:T(8,128)S(1)}, u32[]{:S(2)}, u32[]{:S(2)}) collective-permute-start(f32[16,512]{1,0:T(8,128)S(1)} %get-tuple-element.51.last_ref), channel_id=1, source_target_pairs={{0,16},{8,24},{16,0},{24,8},{32,48},{40,56},{48,32},{56,40},{64,80... | collective-permute-start | bytes 98312 | tf_op jit(solution)/shard_map/ppermute | solution.py:455
  10.7 16.4 %collective-permute-start = (f32[16,512]{1,0:T(8,128)S(1)}, f32[16,512]{1,0:T(8,128)S(1)}, u32[]{:S(2)}, u32[]{:S(2)}) collective-permute-start(f32[16,512]{1,0:T(8,128)S(1)} %get-tuple-element.51.last_ref), channel_id=1, source_target_pairs={{0,8},{8,0},{16,24},{24,16},{32,40},{40,32},{48,56},{56,48},{64,72... | collective-permute-start | bytes 98312 | tf_op jit(solution)/shard_map/ppermute | solution.py:455
  27.2 9.9 %collective-permute-start.5 = (f32[16,512]{1,0:T(8,128)S(1)}, f32[16,512]{1,0:T(8,128)S(1)}, u32[]{:S(2)}, u32[]{:S(2)}) collective-permute-start(f32[16,512]{1,0:T(8,128)S(1)} %get-tuple-element.58), channel_id=1, source_target_pairs={{0,96},{8,104},{16,112},{24,120},{1,97},{9,105},{17,113},{25,121},... | collective-permute-start | bytes 98312 | tf_op jit(solution)/shard_map/ppermute | solution.py:458
  32.2 5.0 %collective-permute-start.4 = (f32[16,512]{1,0:T(8,128)S(1)}, f32[16,512]{1,0:T(8,128)S(1)}, u32[]{:S(2)}, u32[]{:S(2)}) collective-permute-start(f32[16,512]{1,0:T(8,128)S(1)} %get-tuple-element.58), channel_id=1, source_target_pairs={{0,64},{8,72},{16,80},{24,88},{32,96},{40,104},{48,112},{56,120},{... | collective-permute-start | bytes 98312 | tf_op jit(solution)/shard_map/ppermute | solution.py:458
  33.5 4.3 %collective-permute-start.3 = (f32[16,512]{1,0:T(8,128)S(1)}, f32[16,512]{1,0:T(8,128)S(1)}, u32[]{:S(2)}, u32[]{:S(2)}) collective-permute-start(f32[16,512]{1,0:T(8,128)S(1)} %get-tuple-element.58), channel_id=1, source_target_pairs={{0,32},{8,40},{16,48},{24,56},{32,64},{40,72},{48,80},{56,88},{64,... | collective-permute-start | bytes 98312 | tf_op jit(solution)/shard_map/ppermute | solution.py:458
  38.2 14.3 %collective-permute-start.14 = (bf16[128,4096]{1,0:T(8,128)(2,1)S(1)}, bf16[128,4096]{1,0:T(8,128)(2,1)S(1)}, u32[]{:S(2)}, u32[]{:S(2)}) collective-permute-start(bf16[128,4096]{1,0:T(8,128)(2,1)S(1)} %collective-permute-done.10.refs_3_), channel_id=1, source_target_pairs={{0,8},{1,9},{2,10},{3,11},{4,12},{5,13},{6,14},{7,15},{8,0},{9,1},... | collective-permute-start | bytes 3145736 | tf_op jit(solution)/shard_map/ppermute | solution.py:286
  38.4 9.3 %collective-permute-start.9 = (bf16[32,4096]{1,0:T(8,128)(2,1)S(1)}, bf16[32,4096]{1,0:T(8,128)(2,1)S(1)}, u32[]{:S(2)}, u32[]{:S(2)}) collective-permute-start(bf16[32,4096]{1,0:T(8,128)(2,1)S(1)} %get-tuple-element.95), channel_id=1, source_target_pairs={{0,96},{1,97},{2,98},{3,99},{4,100},{5,101},{6,102},{7,103},{8,104... | collective-permute-start | bytes 786440 | tf_op jit(solution)/shard_map/ppermute | solution.py:286
  39.5 9.6 %collective-permute-start.8 = (bf16[32,4096]{1,0:T(8,128)(2,1)S(1)}, bf16[32,4096]{1,0:T(8,128)(2,1)S(1)}, u32[]{:S(2)}, u32[]{:S(2)}) collective-permute-start(bf16[32,4096]{1,0:T(8,128)(2,1)S(1)} %get-tuple-element.96), channel_id=1, source_target_pairs={{0,32},{1,33},{2,34},{3,35},{4,36},{5,37},{6,38},{7,39},{8,40},{9,... | collective-permute-start | bytes 786440 | tf_op jit(solution)/shard_map/ppermute | solution.py:286
  40.9 11.7 %collective-permute-start.11 = (bf16[64,4096]{1,0:T(8,128)(2,1)S(1)}, bf16[64,4096]{1,0:T(8,128)(2,1)S(1)}, u32[]{:S(2)}, u32[]{:S(2)}) collective-permute-start(bf16[64,4096]{1,0:T(8,128)(2,1)S(1)} %collective-permute-done.7.refs_0_), channel_id=1, source_target_pairs={{0,8},{1,9},{2,10},{3,11},{4,12},{5,13},{6,14},{7,15},{8,0},{9,1},... | collective-permute-start | bytes 1572872 | tf_op jit(solution)/shard_map/ppermute | solution.py:286
  47.7 1.6 %collective-permute-start.13 = (bf16[32,4096]{1,0:T(8,128)(2,1)S(1)}, bf16[32,4096]{1,0:T(8,128)(2,1)S(1)}, u32[]{:S(2)}, u32[]{:S(2)}) collective-permute-start(bf16[32,4096]{1,0:T(8,128)(2,1)S(1)} %collective-permute-done.9.refs_2_), channel_id=1, source_target_pairs={{0,8},{1,9},{2,10},{3,11},{4,12},{5,13},{6,14},{7,15},{8,0},{9,1},... | collective-permute-start | bytes 786440 | tf_op jit(solution)/shard_map/ppermute | solution.py:286
  49.1 2.0 %collective-permute-start.12 = (bf16[32,4096]{1,0:T(8,128)(2,1)S(1)}, bf16[32,4096]{1,0:T(8,128)(2,1)S(1)}, u32[]{:S(2)}, u32[]{:S(2)}) collective-permute-start(bf16[32,4096]{1,0:T(8,128)(2,1)S(1)} %collective-permute-done.8.refs_1_), channel_id=1, source_target_pairs={{0,8},{1,9},{2,10},{3,11},{4,12},{5,13},{6,14},{7,15},{8,0},{9,1},... | collective-permute-start | bytes 786440 | tf_op jit(solution)/shard_map/ppermute | solution.py:286
  49.1 16.6 %collective-permute-start.15 = (bf16[256,512]{1,0:T(8,128)(2,1)S(1)}, bf16[256,512]{1,0:T(8,128)(2,1)S(1)}, u32[]{:S(2)}, u32[]{:S(2)}) collective-permute-start(bf16[256,512]{1,0:T(8,128)(2,1)S(1)} %get-tuple-element.66), channel_id=1, source_target_pairs={{0,4},{1,5},{2,6},{3,7},{4,0},{5,1},{6,2},{7,3},{8,12},{9,13},{10,... | collective-permute-start | bytes 786440 | tf_op jit(solution)/shard_map/ppermute | solution.py:286
  49.4 11.8 %collective-permute-start.6 = (bf16[128,512]{1,0:T(8,128)(2,1)S(1)}, bf16[128,512]{1,0:T(8,128)(2,1)S(1)}, u32[]{:S(2)}, u32[]{:S(2)}) collective-permute-start(bf16[128,512]{1,0:T(8,128)(2,1)S(1)} %get-tuple-element.63), channel_id=1, source_target_pairs={{0,4},{1,5},{2,6},{3,7},{4,0},{5,1},{6,2},{7,3},{8,12},{9,13},{10,... | collective-permute-start | bytes 393224 | tf_op jit(solution)/shard_map/ppermute | solution.py:286
  51.2 17.1 %collective-permute-start.16 = (bf16[128,512]{1,0:T(8,128)(2,1)S(1)}, bf16[128,512]{1,0:T(8,128)(2,1)S(1)}, u32[]{:S(2)}, u32[]{:S(2)}) collective-permute-start(bf16[128,512]{1,0:T(8,128)(2,1)S(1)} %get-tuple-element.67), channel_id=1, source_target_pairs={{0,4},{1,5},{2,6},{3,7},{4,0},{5,1},{6,2},{7,3},{8,12},{9,13},{10,... | collective-permute-start | bytes 393224 | tf_op jit(solution)/shard_map/ppermute | solution.py:286
  52.5 8.6 %copy-start = (bf16[512,4096]{1,0:T(8,128)(2,1)S(1)}, bf16[512,4096]{1,0:T(8,128)(2,1)}, u32[]{:S(2)}) copy-start(bf16[512,4096]{1,0:T(8,128)(2,1)} %refs_2_.11) | copy-start | bytes 12582916
  61.9 13.0 %collective-permute-start.20 = (bf16[128,512]{1,0:T(8,128)(2,1)S(1)}, bf16[128,512]{1,0:T(8,128)(2,1)S(1)}, u32[]{:S(2)}, u32[]{:S(2)}) collective-permute-start(bf16[128,512]{1,0:T(8,128)(2,1)S(1)} %get-tuple-element.80), channel_id=1, source_target_pairs={{0,1},{1,2},{2,3},{3,0},{4,5},{5,6},{6,7},{7,4},{8,9},{9,10},{10,1... | collective-permute-start | bytes 393224 | tf_op jit(solution)/shard_map/ppermute | solution.py:286
  63.9 42.7 %collective-permute-start.17 = (bf16[128,512]{1,0:T(8,128)(2,1)S(1)}, bf16[128,512]{1,0:T(8,128)(2,1)S(1)}, u32[]{:S(2)}, u32[]{:S(2)}) collective-permute-start(bf16[128,512]{1,0:T(8,128)(2,1)S(1)} %get-tuple-element.70), channel_id=1, source_target_pairs={{0,1},{1,2},{2,3},{3,0},{4,5},{5,6},{6,7},{7,4},{8,9},{9,10},{10,1... | collective-permute-start | bytes 393224 | tf_op jit(solution)/shard_map/ppermute | solution.py:286
  69.8 6.4 %collective-permute-start.18 = (bf16[128,512]{1,0:T(8,128)(2,1)S(1)}, bf16[128,512]{1,0:T(8,128)(2,1)S(1)}, u32[]{:S(2)}, u32[]{:S(2)}) collective-permute-start(bf16[128,512]{1,0:T(8,128)(2,1)S(1)} %get-tuple-element.77), channel_id=1, source_target_pairs={{0,3},{1,0},{2,1},{3,2},{4,7},{5,4},{6,5},{7,6},{8,11},{9,8},{10,9... | collective-permute-start | bytes 393224 | tf_op jit(solution)/shard_map/ppermute | solution.py:286
  71.2 22.9 %collective-permute-start.22 = (bf16[128,512]{1,0:T(8,128)(2,1)S(1)}, bf16[128,512]{1,0:T(8,128)(2,1)S(1)}, u32[]{:S(2)}, u32[]{:S(2)}) collective-permute-start(bf16[128,512]{1,0:T(8,128)(2,1)S(1)} %get-tuple-element.81), channel_id=1, source_target_pairs={{0,3},{1,0},{2,1},{3,2},{4,7},{5,4},{6,5},{7,6},{8,11},{9,8},{10,9... | collective-permute-start | bytes 393224 | tf_op jit(solution)/shard_map/ppermute | solution.py:286
  72.4 21.2 %collective-permute-start.25 = (bf16[256,512]{1,0:T(8,128)(2,1)S(1)}, bf16[256,512]{1,0:T(8,128)(2,1)S(1)}, u32[]{:S(2)}, u32[]{:S(2)}) collective-permute-start(bf16[256,512]{1,0:T(8,128)(2,1)S(1)} %get-tuple-element.83), channel_id=1, source_target_pairs={{0,3},{1,0},{2,1},{3,2},{4,7},{5,4},{6,5},{7,6},{8,11},{9,8},{10,9... | collective-permute-start | bytes 786440 | tf_op jit(solution)/shard_map/ppermute | solution.py:286
  74.9 18.2 %collective-permute-start.27 = (bf16[256,512]{1,0:T(8,128)(2,1)S(1)}, bf16[256,512]{1,0:T(8,128)(2,1)S(1)}, u32[]{:S(2)}, u32[]{:S(2)}) collective-permute-start(bf16[256,512]{1,0:T(8,128)(2,1)S(1)} %get-tuple-element.86), channel_id=1, source_target_pairs={{0,1},{1,2},{2,3},{3,0},{4,5},{5,6},{6,7},{7,4},{8,9},{9,10},{10,1... | collective-permute-start | bytes 786440 | tf_op jit(solution)/shard_map/ppermute | solution.py:286
  76.3 8.9 %collective-permute-start.32 = (bf16[128,512]{1,0:T(8,128)(2,1)S(1)}, bf16[128,512]{1,0:T(8,128)(2,1)S(1)}, u32[]{:S(2)}, u32[]{:S(2)}) collective-permute-start(bf16[128,512]{1,0:T(8,128)(2,1)S(1)} %get-tuple-element.90), channel_id=1, source_target_pairs={{0,3},{1,0},{2,1},{3,2},{4,7},{5,4},{6,5},{7,6},{8,11},{9,8},{10,9... | collective-permute-start | bytes 393224 | tf_op jit(solution)/shard_map/ppermute | solution.py:286
  85.2 6.2 %collective-permute-start.34 = (bf16[128,512]{1,0:T(8,128)(2,1)S(1)}, bf16[128,512]{1,0:T(8,128)(2,1)S(1)}, u32[]{:S(2)}, u32[]{:S(2)}) collective-permute-start(bf16[128,512]{1,0:T(8,128)(2,1)S(1)} %get-tuple-element.93), channel_id=1, source_target_pairs={{0,1},{1,2},{2,3},{3,0},{4,5},{5,6},{6,7},{7,4},{8,9},{9,10},{10,1... | collective-permute-start | bytes 393224 | tf_op jit(solution)/shard_map/ppermute | solution.py:286
  91.3 9.5 %collective-permute-start.29 = (bf16[256,512]{1,0:T(8,128)(2,1)S(1)}, bf16[256,512]{1,0:T(8,128)(2,1)S(1)}, u32[]{:S(2)}, u32[]{:S(2)}) collective-permute-start(bf16[256,512]{1,0:T(8,128)(2,1)S(1)} %get-tuple-element.87), channel_id=1, source_target_pairs={{0,3},{1,0},{2,1},{3,2},{4,7},{5,4},{6,5},{7,6},{8,11},{9,8},{10,9... | collective-permute-start | bytes 786440 | tf_op jit(solution)/shard_map/ppermute | solution.py:286
  93.1 7.7 %collective-permute-start.21 = (bf16[128,512]{1,0:T(8,128)(2,1)S(1)}, bf16[128,512]{1,0:T(8,128)(2,1)S(1)}, u32[]{:S(2)}, u32[]{:S(2)}) collective-permute-start(bf16[128,512]{1,0:T(8,128)(2,1)S(1)} %add_convert_fusion.7), channel_id=1, source_target_pairs={{0,1},{1,2},{2,3},{3,0},{4,5},{5,6},{6,7},{7,4},{8,9},{9,10},{10,1... | collective-permute-start | bytes 393224 | tf_op jit(solution)/shard_map/ppermute | solution.py:286
  93.6 12.8 %collective-permute-start.28 = (bf16[256,512]{1,0:T(8,128)(2,1)S(1)}, bf16[256,512]{1,0:T(8,128)(2,1)S(1)}, u32[]{:S(2)}, u32[]{:S(2)}) collective-permute-start(bf16[256,512]{1,0:T(8,128)(2,1)S(1)} %add_convert_fusion.1), channel_id=1, source_target_pairs={{0,1},{1,2},{2,3},{3,0},{4,5},{5,6},{6,7},{7,4},{8,9},{9,10},{10,1... | collective-permute-start | bytes 786440 | tf_op jit(solution)/shard_map/ppermute | solution.py:286
  94.1 19.6 %collective-permute-start.24 = (bf16[256,512]{1,0:T(8,128)(2,1)S(1)}, bf16[256,512]{1,0:T(8,128)(2,1)S(1)}, u32[]{:S(2)}, u32[]{:S(2)}) collective-permute-start(bf16[256,512]{1,0:T(8,128)(2,1)S(1)} %get-tuple-element.73), channel_id=1, source_target_pairs={{0,1},{1,2},{2,3},{3,0},{4,5},{5,6},{6,7},{7,4},{8,9},{9,10},{10,1... | collective-permute-start | bytes 786440 | tf_op jit(solution)/shard_map/ppermute | solution.py:286
  100.8 12.3 %collective-permute-start.31 = (bf16[128,512]{1,0:T(8,128)(2,1)S(1)}, bf16[128,512]{1,0:T(8,128)(2,1)S(1)}, u32[]{:S(2)}, u32[]{:S(2)}) collective-permute-start(bf16[128,512]{1,0:T(8,128)(2,1)S(1)} %get-tuple-element.88), channel_id=1, source_target_pairs={{0,1},{1,2},{2,3},{3,0},{4,5},{5,6},{6,7},{7,4},{8,9},{9,10},{10,1... | collective-permute-start | bytes 393224 | tf_op jit(solution)/shard_map/ppermute | solution.py:286
  100.9 9.0 %collective-permute-start.36 = (bf16[128,512]{1,0:T(8,128)(2,1)S(1)}, bf16[128,512]{1,0:T(8,128)(2,1)S(1)}, u32[]{:S(2)}, u32[]{:S(2)}) collective-permute-start(bf16[128,512]{1,0:T(8,128)(2,1)S(1)} %get-tuple-element.94), channel_id=1, source_target_pairs={{0,3},{1,0},{2,1},{3,2},{4,7},{5,4},{6,5},{7,6},{8,11},{9,8},{10,9... | collective-permute-start | bytes 393224 | tf_op jit(solution)/shard_map/ppermute | solution.py:286
  106.4 6.2 %collective-permute-start.35 = (bf16[128,512]{1,0:T(8,128)(2,1)S(1)}, bf16[128,512]{1,0:T(8,128)(2,1)S(1)}, u32[]{:S(2)}, u32[]{:S(2)}) collective-permute-start(bf16[128,512]{1,0:T(8,128)(2,1)S(1)} %add_convert_fusion.4), channel_id=1, source_target_pairs={{0,1},{1,2},{2,3},{3,0},{4,5},{5,6},{6,7},{7,4},{8,9},{9,10},{10,1... | collective-permute-start | bytes 393224 | tf_op jit(solution)/shard_map/ppermute | solution.py:286
  106.5 8.7 %collective-permute-start.19 = (bf16[128,512]{1,0:T(8,128)(2,1)S(1)}, bf16[128,512]{1,0:T(8,128)(2,1)S(1)}, u32[]{:S(2)}, u32[]{:S(2)}) collective-permute-start(bf16[128,512]{1,0:T(8,128)(2,1)S(1)} %add_convert_fusion.8), channel_id=1, source_target_pairs={{0,3},{1,0},{2,1},{3,2},{4,7},{5,4},{6,5},{7,6},{8,11},{9,8},{10,9... | collective-permute-start | bytes 393224 | tf_op jit(solution)/shard_map/ppermute | solution.py:286
  109.8 11.9 %collective-permute-start.26 = (bf16[256,512]{1,0:T(8,128)(2,1)S(1)}, bf16[256,512]{1,0:T(8,128)(2,1)S(1)}, u32[]{:S(2)}, u32[]{:S(2)}) collective-permute-start(bf16[256,512]{1,0:T(8,128)(2,1)S(1)} %add_convert_fusion.2), channel_id=1, source_target_pairs={{0,3},{1,0},{2,1},{3,2},{4,7},{5,4},{6,5},{7,6},{8,11},{9,8},{10,9... | collective-permute-start | bytes 786440 | tf_op jit(solution)/shard_map/ppermute | solution.py:286
  112.6 9.2 %collective-permute-start.30 = (bf16[256,512]{1,0:T(8,128)(2,1)S(1)}, bf16[256,512]{1,0:T(8,128)(2,1)S(1)}, u32[]{:S(2)}, u32[]{:S(2)}) collective-permute-start(bf16[256,512]{1,0:T(8,128)(2,1)S(1)} %add_convert_fusion), channel_id=1, source_target_pairs={{0,4},{1,5},{2,6},{3,7},{4,0},{5,1},{6,2},{7,3},{8,12},{9,13},{10,... | collective-permute-start | bytes 786440 | tf_op jit(solution)/shard_map/ppermute | solution.py:286
  113.1 5.0 %collective-permute-start.33 = (bf16[128,512]{1,0:T(8,128)(2,1)S(1)}, bf16[128,512]{1,0:T(8,128)(2,1)S(1)}, u32[]{:S(2)}, u32[]{:S(2)}) collective-permute-start(bf16[128,512]{1,0:T(8,128)(2,1)S(1)} %add_convert_fusion.5), channel_id=1, source_target_pairs={{0,3},{1,0},{2,1},{3,2},{4,7},{5,4},{6,5},{7,6},{8,11},{9,8},{10,9... | collective-permute-start | bytes 393224 | tf_op jit(solution)/shard_map/ppermute | solution.py:286
  113.7 6.7 %collective-permute-start.23 = (bf16[128,512]{1,0:T(8,128)(2,1)S(1)}, bf16[128,512]{1,0:T(8,128)(2,1)S(1)}, u32[]{:S(2)}, u32[]{:S(2)}) collective-permute-start(bf16[128,512]{1,0:T(8,128)(2,1)S(1)} %add_convert_fusion.6), channel_id=1, source_target_pairs={{0,4},{1,5},{2,6},{3,7},{4,0},{5,1},{6,2},{7,3},{8,12},{9,13},{10,... | collective-permute-start | bytes 393224 | tf_op jit(solution)/shard_map/ppermute | solution.py:286
  115.2 6.5 %collective-permute-start.37 = (bf16[128,512]{1,0:T(8,128)(2,1)S(1)}, bf16[128,512]{1,0:T(8,128)(2,1)S(1)}, u32[]{:S(2)}, u32[]{:S(2)}) collective-permute-start(bf16[128,512]{1,0:T(8,128)(2,1)S(1)} %add_convert_fusion.3), channel_id=1, source_target_pairs={{0,4},{1,5},{2,6},{3,7},{4,0},{5,1},{6,2},{7,3},{8,12},{9,13},{10,... | collective-permute-start | bytes 393224 | tf_op jit(solution)/shard_map/ppermute | solution.py:286
